TPU v7x, 512 devices: a whole 4x4x16 slice. The times are simulated.
512 devices in a mesh: gx: 32 (over y, x, z_hi), gy: 8 (over z_lo), gz: 2 (over core).
Axes of the slice: x: 4, y: 4, z: 16 (z_hi: 2, z_lo: 8; z = z_hi * 8 + z_lo), core: 2. Of those that a mesh axis runs over, the one named last changes fastest.
Arguments:
- source: float32 [256, 64, 4096], P('gx', 'gz', 'gy'), may hold values from -24 to 24
- coef: float32 [256, 64, 128], P('gx', 'gz', 'gy'), may hold values from 0.01 to 0.05
- face_trace: int32 [256, 2, 128], P('gx', 'gz'), may hold values from 0 to 1023, as said below
- near_col: int32 [32, 2, 8], P('gx', 'gz', 'gy'), may hold values from 0 to 63, as said below
- far_col: int32 [32, 2, 8, 7], P('gx', 'gz', 'gy'), may hold values from 0 to 63, as said below
- near_tile: bfloat16 [32, 2, 8, 1024, 1024], P('gx', 'gz', 'gy'), may hold values from -0.1875 to 0.1875
- far_u: bfloat16 [32, 2, 8, 7, 16, 1024], P('gx', 'gz', 'gy'), may hold values from -0.1875 to 0.1875
- far_v: bfloat16 [32, 2, 8, 7, 16, 1024], P('gx', 'gz', 'gy'), may hold values from -0.1875 to 0.1875
Outputs:
- solution: float32 [256, 64, 4096], P('gx', 'gz', 'gy')
- flux: float32 [256, 2, 4096], P('gx', 'gz', 'gy')
Inputs may be any that keep to these rules, and one draw needn't show every extreme that they name: For every block of 8 rows of x and each face s, the entries face_trace(x, s, y) of that block are a permutation of 0 to 1023. For every row block, near_col over the slots j together with far_col over j and k name each column block 0 to 63 exactly once. `far_col`: see near_col: near and far column blocks of a row block together name every column block exactly once.
All inputs are finite; a program needn't handle non-finite values.
Results may differ from a plain program's by a relative error of at most 0.003.
Values may be sent and summed in bfloat16 or wider, within the bound.
A program may use at most 64 MiB of HBM per device.

v0:
```python
import jax
import jax.numpy as jnp
from jax import lax
from jax.sharding import PartitionSpec as P

E = 32
SWEEPS = 3


def extended(block, sides, width):
    for axis, dim in sides:
        count = lax.axis_size(axis)
        forward = [(i, i + 1) for i in range(count - 1)]
        backward = [(target, source) for source, target in forward]
        low = lax.ppermute(
            lax.slice_in_dim(block, block.shape[dim] - width, None, axis=dim), axis, forward
        )
        high = lax.ppermute(lax.slice_in_dim(block, 0, width, axis=dim), axis, backward)
        block = jnp.concatenate([low, block, high], axis=dim)
    return block


def sweep(field, rhs, diag):
    slab = extended(field, (("gx", 0), ("gz", 1)), 1)
    pencil = extended(field, (("gy", 2),), E)
    beside = slab[2:, 1:-1] + slab[:-2, 1:-1] + slab[1:-1, 2:] + slab[1:-1, :-2]
    beside = beside + pencil[:, :, 2 * E :] + pencil[:, :, : -2 * E]
    return (rhs + beside) / diag


def body(source, coef, face_trace, near_col, far_col, near_tile, far_u, far_v):
    rows_x = source.shape[0]
    depth = source.shape[1]
    cells_y = coef.shape[2]
    groups = lax.axis_size("gy")
    mine_y = lax.axis_index("gy")
    face_side = lax.axis_index("gz")
    tile = near_tile.shape[3]
    far_count = far_u.shape[3]
    rank = far_u.shape[4]
    diag = jnp.repeat(6.0 + coef, E, axis=2)
    field = jnp.zeros(source.shape, jnp.float32)
    for step in range(SWEEPS):
        field = sweep(field, source, diag)
    plane = jnp.where(face_side == 0, 0, depth - 1)
    depth_ids = jnp.arange(depth, dtype=jnp.int32)
    plane_mask = (depth_ids == plane).astype(jnp.float32)
    face_local = jnp.where(face_side == 0, field[:, 0, :], field[:, depth - 1, :]).astype(
        jnp.bfloat16
    )
    face_block = lax.all_gather(face_local, "gy", axis=1, tiled=True)
    perm = face_trace.reshape(tile)
    inverse = jnp.zeros((tile,), jnp.int32).at[perm].set(jnp.arange(tile, dtype=jnp.int32))
    block_traces = face_block.reshape(tile, E)[inverse].T
    wanted = jnp.concatenate([near_col.reshape(1), far_col.reshape(far_count)])
    piece = lax.all_gather(block_traces[None], ("gx", "gz"), axis=0, tiled=True)
    numbers = jnp.arange(piece.shape[0], dtype=jnp.int32)
    onehot = (wanted[:, None] == numbers[None, :]).astype(jnp.bfloat16)
    chosen = jnp.einsum("cn,net->cet", onehot, piece, preferred_element_type=jnp.float32).astype(
        jnp.bfloat16
    )
    nearpart = lax.dot_general(
        chosen[0],
        near_tile.reshape(tile, tile),
        (((1,), (1,)), ((), ())),
        preferred_element_type=jnp.float32,
    )
    weights = jnp.einsum(
        "fet,frt->fer",
        chosen[1:],
        far_v.reshape(far_count, rank, tile),
        preferred_element_type=jnp.float32,
    ).astype(jnp.bfloat16)
    farpart = jnp.einsum(
        "fer,frt->et",
        weights,
        far_u.reshape(far_count, rank, tile),
        preferred_element_type=jnp.float32,
    )
    partial_rows = nearpart + farpart
    total = lax.psum(partial_rows, "gy")
    face_flux = total[:, perm].reshape(E, rows_x, cells_y * groups)
    mine = lax.dynamic_slice_in_dim(face_flux, mine_y * cells_y, cells_y, 2)
    flux_rows = mine.transpose(1, 2, 0).reshape(rows_x, cells_y * E)
    extra = plane_mask[None, :, None] * flux_rows[:, None, :]
    solution = sweep(field, source + extra, diag)
    return (solution, flux_rows[:, None, :])


def solution(mesh):
    return jax.shard_map(
        body,
        mesh=mesh,
        in_specs=(
            P("gx", "gz", "gy"),
            P("gx", "gz", "gy"),
            P("gx", "gz", None),
            P("gx", "gz", "gy"),
            P("gx", "gz", "gy", None),
            P("gx", "gz", "gy", None, None),
            P("gx", "gz", "gy", None, None, None),
            P("gx", "gz", "gy", None, None, None),
        ),
        out_specs=(P("gx", "gz", "gy"), P("gx", "gz", "gy")),
        check_vma=False,
    )
```

profile of v0, /device:TPU:24, one launch (start us, length us, event | category | flops | bytes accessed | tf_op | source)
XLA Modules:
  0.0 448.6 jit_solution(9452833639911425397)
XLA Ops:
  7.2 18.2 %collective-permute-start = (f32[1,32,512]{2,1,0:T(8,128)S(1)}, f32[1,32,512]{2,1,0:T(8,128)S(1)}, u32[]{:S(2)}, u32[]{:S(2)}) collective-permute-start(f32[1,32,512]{2,1,0:T(8,128)S(1)} %broadcast.45), channel_id=1, source_target_pairs={{16,0},{32,16},{48,32},{64,48},{80,64},{96,80},{112,96},{128,112},... | collective-permute-start | bytes 196616 | tf_op jit(solution)/shard_map/ppermute | solution.py:18
  29.4 5.2 %collective-permute-start.5 = (f32[8,32,32]{2,1,0:T(8,128)}, f32[8,32,32]{2,1,0:T(8,128)}, u32[]{:S(2)}, u32[]{:S(2)}) collective-permute-start(f32[8,32,32]{2,1,0:T(8,128)} %broadcast.46), channel_id=1, source_target_pairs={{0,2},{2,4},{4,6},{6,8},{8,10},{10,12},{12,14},{1,3},{3,5},{5,7},{... | collective-permute-start | bytes 98312 | tf_op jit(solution)/shard_map/ppermute | solution.py:15
  34.6 10.4 %collective-permute-done.1 = f32[1,32,512]{2,1,0:T(8,128)S(1)} collective-permute-done((f32[1,32,512]{2,1,0:T(8,128)S(1)}, f32[1,32,512]{2,1,0:T(8,128)S(1)}, u32[]{:S(2)}, u32[]{:S(2)}) %collective-permute-start.1) | collective-permute-done | bytes 65568 | tf_op jit(solution)/shard_map/ppermute | solution.py:15
  46.3 3.0 collective-permute-start.3
  56.3 5.3 %collective-permute-start.6 = (f32[1,32,512]{2,1,0:T(8,128)S(1)}, f32[1,32,512]{2,1,0:T(8,128)S(1)}, u32[]{:S(2)}, u32[]{:S(2)}) collective-permute-start(f32[1,32,512]{2,1,0:T(8,128)S(1)} %get-tuple-element.19), channel_id=1, source_target_pairs={{16,0},{32,16},{48,32},{64,48},{80,64},{96,80},{112,96},{128,112},... | collective-permute-start | bytes 196616 | tf_op jit(solution)/shard_map/ppermute | solution.py:18
  61.6 9.3 %collective-permute-start.7 = (f32[1,32,512]{2,1,0:T(8,128)S(1)}, f32[1,32,512]{2,1,0:T(8,128)S(1)}, u32[]{:S(2)}, u32[]{:S(2)}) collective-permute-start(f32[1,32,512]{2,1,0:T(8,128)S(1)} %get-tuple-element.18), channel_id=1, source_target_pairs={{0,16},{16,32},{32,48},{48,64},{64,80},{80,96},{96,112},{112,128},... | collective-permute-start | bytes 196616 | tf_op jit(solution)/shard_map/ppermute | solution.py:15
  72.9 4.6 %collective-permute-start.11 = (f32[8,32,32]{2,1,0:T(8,128)}, f32[8,32,32]{2,1,0:T(8,128)S(1)}, u32[]{:S(2)}, u32[]{:S(2)}) collective-permute-start(f32[8,32,32]{2,1,0:T(8,128)} %get-tuple-element.21), channel_id=1, source_target_pairs={{0,2},{2,4},{4,6},{6,8},{8,10},{10,12},{12,14},{1,3},{3,5},{5,7},{... | collective-permute-start | bytes 98312 | tf_op jit(solution)/shard_map/ppermute | solution.py:15
  82.0 4.2 collective-permute-start.9
  86.9 4.3 scatter_custom_fusion
  94.2 6.6 %collective-permute-start.12 = (f32[1,32,512]{2,1,0:T(8,128)S(1)}, f32[1,32,512]{2,1,0:T(8,128)S(1)}, u32[]{:S(2)}, u32[]{:S(2)}) collective-permute-start(f32[1,32,512]{2,1,0:T(8,128)S(1)} %get-tuple-element.15), channel_id=1, source_target_pairs={{16,0},{32,16},{48,32},{64,48},{80,64},{96,80},{112,96},{128,112},... | collective-permute-start | bytes 196616 | tf_op jit(solution)/shard_map/ppermute | solution.py:18
  100.8 7.9 %collective-permute-start.13 = (f32[1,32,512]{2,1,0:T(8,128)S(1)}, f32[1,32,512]{2,1,0:T(8,128)S(1)}, u32[]{:S(2)}, u32[]{:S(2)}) collective-permute-start(f32[1,32,512]{2,1,0:T(8,128)S(1)} %get-tuple-element.14), channel_id=1, source_target_pairs={{0,16},{16,32},{32,48},{48,64},{64,80},{80,96},{96,112},{112,128},... | collective-permute-start | bytes 196616 | tf_op jit(solution)/shard_map/ppermute | solution.py:15
  110.8 7.2 %collective-permute-start.17 = (f32[8,32,32]{2,1,0:T(8,128)}, f32[8,32,32]{2,1,0:T(8,128)S(1)}, u32[]{:S(2)}, u32[]{:S(2)}) collective-permute-start(f32[8,32,32]{2,1,0:T(8,128)} %get-tuple-element.17), channel_id=1, source_target_pairs={{0,2},{2,4},{4,6},{6,8},{8,10},{10,12},{12,14},{1,3},{3,5},{5,7},{... | collective-permute-start | bytes 98312 | tf_op jit(solution)/shard_map/ppermute | solution.py:15
  120.8 4.2 collective-permute-start.15
  129.3 42.8 %all-gather = bf16[8,1,4096]{2,1,0:T(2,128)(2,1)S(1)} all-gather(bf16[8,1,512]{2,1,0:T(2,128)(2,1)S(1)} %fusion.43), channel_id=2, replica_groups=mesh['gx'=32,'gy'=8,'gz'=2] {'gy'}, dimensions={2}, use_global_device_ids=true | all-gather | bytes 73728 | tf_op jit(solution)/shard_map/all_gather | solution.py:51
  172.7 4.3 gather_fusion
  181.1 6.2 %collective-permute-start.18 = (f32[1,32,512]{2,1,0:T(8,128)}, f32[1,32,512]{2,1,0:T(8,128)S(1)}, u32[]{:S(2)}, u32[]{:S(2)}) collective-permute-start(f32[1,32,512]{2,1,0:T(8,128)} %get-tuple-element.11), channel_id=1, source_target_pairs={{16,0},{32,16},{48,32},{64,48},{80,64},{96,80},{112,96},{128,112},... | collective-permute-start | bytes 196616 | tf_op jit(solution)/shard_map/ppermute | solution.py:18
  187.3 8.5 %collective-permute-start.19 = (f32[1,32,512]{2,1,0:T(8,128)}, f32[1,32,512]{2,1,0:T(8,128)S(1)}, u32[]{:S(2)}, u32[]{:S(2)}) collective-permute-start(f32[1,32,512]{2,1,0:T(8,128)} %get-tuple-element.10), channel_id=1, source_target_pairs={{0,16},{16,32},{32,48},{48,64},{64,80},{80,96},{96,112},{112,128},... | collective-permute-start | bytes 196616 | tf_op jit(solution)/shard_map/ppermute | solution.py:15
  195.8 109.5 %all-gather.4.cloned.1.call-done = bf16[2048,1024]{1,0:T(8,128)(2,1)} async-done(((bf16[32,1024]{1,0:T(8,128)(2,1)}), bf16[2048,1024]{1,0:T(8,128)(2,1)}) %all-gather.4.cloned.1.call-update) | async-done | bytes 4194320 | tf_op jit(solution)/shard_map/all_gather | solution.py:56
  305.3 6.7 %fusion.4 = bf16[8,32,1024]{2,0,1:T(8,128)(2,1)S(1)} fusion(bf16[64,32,1024]{2,1,0:T(8,128)(2,1)} %bitcast.35, s32[8]{0:T(128)S(1)} %pad_add_fusion), kind=kOutput, calls=%fused_computation.7 | convolution fusion | flops 33817088 | bytes 4718624 | tf_op jit(solution)/shard_map/cn,net->cet/dot_general | solution.py:59
  319.3 5.2 %collective-permute-start.23 = (f32[8,32,32]{2,1,0:T(8,128)}, f32[8,32,32]{2,1,0:T(8,128)}, u32[]{:S(2)}, u32[]{:S(2)}) collective-permute-start(f32[8,32,32]{2,1,0:T(8,128)} %get-tuple-element.13), channel_id=1, source_target_pairs={{0,2},{2,4},{4,6},{6,8},{8,10},{10,12},{12,14},{1,3},{3,5},{5,7},{... | collective-permute-start | bytes 98312 | tf_op jit(solution)/shard_map/ppermute | solution.py:15
  327.4 3.0 collective-permute-start.21
  330.4 99.0 %all-reduce.6.cloned.1.call-done = f32[32,1024]{1,0:T(8,128)} async-done(((f32[32,1024]{1,0:T(8,128)}), f32[32,1024]{1,0:T(8,128)}) %all-reduce.6.cloned.1.call-update) | async-done | bytes 131088 | tf_op jit(solution)/shard_map/psum | solution.py:81
  431.3 5.0 %gather_fusion.1 = f32[1024,32]{1,0:T(8,128)} fusion(f32[32,1024]{0,1:T(8,128)} %copy.20, s32[1024]{0:T(1024)S(1)} %broadcast_clamp_fusion), kind=kCustom, calls=%fused_computation.1 | custom fusion | bytes 266240 | tf_op jit(solution)/shard_map/gather | solution.py:82
  438.0 3.8 fusion.17
  (88 shorter events, 49.0 us)
Async XLA Ops:
  7.2 298.1 %all-gather.4.cloned.1.call-start = ((), (), s32[]{:S(2)}) async-start(), calls=%async_computation.1 | async-start | bytes 4259840 | tf_op jit(solution)/shard_map/all_gather | solution.py:56
  7.2 27.3 %collective-permute-start = (f32[1,32,512]{2,1,0:T(8,128)S(1)}, f32[1,32,512]{2,1,0:T(8,128)S(1)}, u32[]{:S(2)}, u32[]{:S(2)}) collective-permute-start(f32[1,32,512]{2,1,0:T(8,128)S(1)} %broadcast.45), channel_id=1, source_target_pairs={{16,0},{32,16},{48,32},{64,48},{80,64},{96,80},{112,96},{128,112},... | collective-permute-start | bytes 196616 | tf_op jit(solution)/shard_map/ppermute | solution.py:18
  25.5 19.5 %collective-permute-start.1 = (f32[1,32,512]{2,1,0:T(8,128)S(1)}, f32[1,32,512]{2,1,0:T(8,128)S(1)}, u32[]{:S(2)}, u32[]{:S(2)}) collective-permute-start(f32[1,32,512]{2,1,0:T(8,128)S(1)} %broadcast.45), channel_id=1, source_target_pairs={{0,16},{16,32},{32,48},{48,64},{64,80},{80,96},{96,112},{112,128},... | collective-permute-start | bytes 196616 | tf_op jit(solution)/shard_map/ppermute | solution.py:15
  28.1 26.5 %collective-permute-start.4 = (f32[8,32,32]{2,1,0:T(8,128)}, f32[8,32,32]{2,1,0:T(8,128)}, u32[]{:S(2)}, u32[]{:S(2)}) collective-permute-start(f32[8,32,32]{2,1,0:T(8,128)} %broadcast.46), channel_id=1, source_target_pairs={{2,0},{4,2},{6,4},{8,6},{10,8},{12,10},{14,12},{3,1},{5,3},{7,5},{... | collective-permute-start | bytes 98312 | tf_op jit(solution)/shard_map/ppermute | solution.py:18
  29.4 25.3 %collective-permute-start.5 = (f32[8,32,32]{2,1,0:T(8,128)}, f32[8,32,32]{2,1,0:T(8,128)}, u32[]{:S(2)}, u32[]{:S(2)}) collective-permute-start(f32[8,32,32]{2,1,0:T(8,128)} %broadcast.46), channel_id=1, source_target_pairs={{0,2},{2,4},{4,6},{6,8},{8,10},{10,12},{12,14},{1,3},{3,5},{5,7},{... | collective-permute-start | bytes 98312 | tf_op jit(solution)/shard_map/ppermute | solution.py:15
  45.0 9.6 %collective-permute-start.2 = (f32[10,1,512]{2,1,0:T(1,128)S(1)}, f32[10,1,512]{2,1,0:T(1,128)S(1)}, u32[]{:S(2)}, u32[]{:S(2)}) collective-permute-start(f32[10,1,512]{2,1,0:T(1,128)S(1)} %get-tuple-element.8), channel_id=1, source_target_pairs={{1,0},{3,2},{5,4},{7,6},{9,8},{11,10},{13,12},{15,14},{17,16},{19,... | collective-permute-start | bytes 61448 | tf_op jit(solution)/shard_map/ppermute | solution.py:18
  46.3 8.3 %collective-permute-start.3 = (f32[10,1,512]{2,1,0:T(1,128)S(1)}, f32[10,1,512]{2,1,0:T(1,128)S(1)}, u32[]{:S(2)}, u32[]{:S(2)}) collective-permute-start(f32[10,1,512]{2,1,0:T(1,128)S(1)} %get-tuple-element.9), channel_id=1, source_target_pairs={{0,1},{2,3},{4,5},{6,7},{8,9},{10,11},{12,13},{14,15},{16,17},{18,... | collective-permute-start | bytes 61448 | tf_op jit(solution)/shard_map/ppermute | solution.py:15
  56.3 21.2 %collective-permute-start.6 = (f32[1,32,512]{2,1,0:T(8,128)S(1)}, f32[1,32,512]{2,1,0:T(8,128)S(1)}, u32[]{:S(2)}, u32[]{:S(2)}) collective-permute-start(f32[1,32,512]{2,1,0:T(8,128)S(1)} %get-tuple-element.19), channel_id=1, source_target_pairs={{16,0},{32,16},{48,32},{64,48},{80,64},{96,80},{112,96},{128,112},... | collective-permute-start | bytes 196616 | tf_op jit(solution)/shard_map/ppermute | solution.py:18
  61.6 18.4 %collective-permute-start.7 = (f32[1,32,512]{2,1,0:T(8,128)S(1)}, f32[1,32,512]{2,1,0:T(8,128)S(1)}, u32[]{:S(2)}, u32[]{:S(2)}) collective-permute-start(f32[1,32,512]{2,1,0:T(8,128)S(1)} %get-tuple-element.18), channel_id=1, source_target_pairs={{0,16},{16,32},{32,48},{48,64},{64,80},{80,96},{96,112},{112,128},... | collective-permute-start | bytes 196616 | tf_op jit(solution)/shard_map/ppermute | solution.py:15
  71.7 19.6 %collective-permute-start.10 = (f32[8,32,32]{2,1,0:T(8,128)}, f32[8,32,32]{2,1,0:T(8,128)S(1)}, u32[]{:S(2)}, u32[]{:S(2)}) collective-permute-start(f32[8,32,32]{2,1,0:T(8,128)} %get-tuple-element.20), channel_id=1, source_target_pairs={{2,0},{4,2},{6,4},{8,6},{10,8},{12,10},{14,12},{3,1},{5,3},{7,5},{... | collective-permute-start | bytes 98312 | tf_op jit(solution)/shard_map/ppermute | solution.py:18
  72.9 18.3 %collective-permute-start.11 = (f32[8,32,32]{2,1,0:T(8,128)}, f32[8,32,32]{2,1,0:T(8,128)S(1)}, u32[]{:S(2)}, u32[]{:S(2)}) collective-permute-start(f32[8,32,32]{2,1,0:T(8,128)} %get-tuple-element.21), channel_id=1, source_target_pairs={{0,2},{2,4},{4,6},{6,8},{8,10},{10,12},{12,14},{1,3},{3,5},{5,7},{... | collective-permute-start | bytes 98312 | tf_op jit(solution)/shard_map/ppermute | solution.py:15
  80.7 10.5 %collective-permute-start.8 = (f32[10,1,512]{2,1,0:T(1,128)}, f32[10,1,512]{2,1,0:T(1,128)}, u32[]{:S(2)}, u32[]{:S(2)}) collective-permute-start(f32[10,1,512]{2,1,0:T(1,128)} %get-tuple-element.6), channel_id=1, source_target_pairs={{1,0},{3,2},{5,4},{7,6},{9,8},{11,10},{13,12},{15,14},{17,16},{19,... | collective-permute-start | bytes 61448 | tf_op jit(solution)/shard_map/ppermute | solution.py:18
  82.0 9.3 %collective-permute-start.9 = (f32[10,1,512]{2,1,0:T(1,128)}, f32[10,1,512]{2,1,0:T(1,128)}, u32[]{:S(2)}, u32[]{:S(2)}) collective-permute-start(f32[10,1,512]{2,1,0:T(1,128)} %get-tuple-element.7), channel_id=1, source_target_pairs={{0,1},{2,3},{4,5},{6,7},{8,9},{10,11},{12,13},{14,15},{16,17},{18,... | collective-permute-start | bytes 61448 | tf_op jit(solution)/shard_map/ppermute | solution.py:15
  94.2 23.8 %collective-permute-start.12 = (f32[1,32,512]{2,1,0:T(8,128)S(1)}, f32[1,32,512]{2,1,0:T(8,128)S(1)}, u32[]{:S(2)}, u32[]{:S(2)}) collective-permute-start(f32[1,32,512]{2,1,0:T(8,128)S(1)} %get-tuple-element.15), channel_id=1, source_target_pairs={{16,0},{32,16},{48,32},{64,48},{80,64},{96,80},{112,96},{128,112},... | collective-permute-start | bytes 196616 | tf_op jit(solution)/shard_map/ppermute | solution.py:18
  100.8 18.1 %collective-permute-start.13 = (f32[1,32,512]{2,1,0:T(8,128)S(1)}, f32[1,32,512]{2,1,0:T(8,128)S(1)}, u32[]{:S(2)}, u32[]{:S(2)}) collective-permute-start(f32[1,32,512]{2,1,0:T(8,128)S(1)} %get-tuple-element.14), channel_id=1, source_target_pairs={{0,16},{16,32},{32,48},{48,64},{64,80},{80,96},{96,112},{112,128},... | collective-permute-start | bytes 196616 | tf_op jit(solution)/shard_map/ppermute | solution.py:15
  109.5 15.5 %collective-permute-start.16 = (f32[8,32,32]{2,1,0:T(8,128)}, f32[8,32,32]{2,1,0:T(8,128)S(1)}, u32[]{:S(2)}, u32[]{:S(2)}) collective-permute-start(f32[8,32,32]{2,1,0:T(8,128)} %get-tuple-element.16), channel_id=1, source_target_pairs={{2,0},{4,2},{6,4},{8,6},{10,8},{12,10},{14,12},{3,1},{5,3},{7,5},{... | collective-permute-start | bytes 98312 | tf_op jit(solution)/shard_map/ppermute | solution.py:18
  110.8 14.2 %collective-permute-start.17 = (f32[8,32,32]{2,1,0:T(8,128)}, f32[8,32,32]{2,1,0:T(8,128)S(1)}, u32[]{:S(2)}, u32[]{:S(2)}) collective-permute-start(f32[8,32,32]{2,1,0:T(8,128)} %get-tuple-element.17), channel_id=1, source_target_pairs={{0,2},{2,4},{4,6},{6,8},{8,10},{10,12},{12,14},{1,3},{3,5},{5,7},{... | collective-permute-start | bytes 98312 | tf_op jit(solution)/shard_map/ppermute | solution.py:15
  178.7 250.7 %all-reduce.6.cloned.1.call-start = ((), (), s32[]{:S(2)}) async-start(), calls=%async_computation | async-start | bytes 262144 | tf_op jit(solution)/shard_map/psum | solution.py:81
  181.1 143.4 %collective-permute-start.18 = (f32[1,32,512]{2,1,0:T(8,128)}, f32[1,32,512]{2,1,0:T(8,128)S(1)}, u32[]{:S(2)}, u32[]{:S(2)}) collective-permute-start(f32[1,32,512]{2,1,0:T(8,128)} %get-tuple-element.11), channel_id=1, source_target_pairs={{16,0},{32,16},{48,32},{64,48},{80,64},{96,80},{112,96},{128,112},... | collective-permute-start | bytes 196616 | tf_op jit(solution)/shard_map/ppermute | solution.py:18
  187.3 137.2 %collective-permute-start.19 = (f32[1,32,512]{2,1,0:T(8,128)}, f32[1,32,512]{2,1,0:T(8,128)S(1)}, u32[]{:S(2)}, u32[]{:S(2)}) collective-permute-start(f32[1,32,512]{2,1,0:T(8,128)} %get-tuple-element.10), channel_id=1, source_target_pairs={{0,16},{16,32},{32,48},{48,64},{64,80},{80,96},{96,112},{112,128},... | collective-permute-start | bytes 196616 | tf_op jit(solution)/shard_map/ppermute | solution.py:15
  318.0 120.0 %collective-permute-start.22 = (f32[8,32,32]{2,1,0:T(8,128)}, f32[8,32,32]{2,1,0:T(8,128)S(1)}, u32[]{:S(2)}, u32[]{:S(2)}) collective-permute-start(f32[8,32,32]{2,1,0:T(8,128)} %get-tuple-element.12), channel_id=1, source_target_pairs={{2,0},{4,2},{6,4},{8,6},{10,8},{12,10},{14,12},{3,1},{5,3},{7,5},{... | collective-permute-start | bytes 98312 | tf_op jit(solution)/shard_map/ppermute | solution.py:18
  319.3 118.7 %collective-permute-start.23 = (f32[8,32,32]{2,1,0:T(8,128)}, f32[8,32,32]{2,1,0:T(8,128)}, u32[]{:S(2)}, u32[]{:S(2)}) collective-permute-start(f32[8,32,32]{2,1,0:T(8,128)} %get-tuple-element.13), channel_id=1, source_target_pairs={{0,2},{2,4},{4,6},{6,8},{8,10},{10,12},{12,14},{1,3},{3,5},{5,7},{... | collective-permute-start | bytes 98312 | tf_op jit(solution)/shard_map/ppermute | solution.py:15
  326.1 111.9 %collective-permute-start.20 = (f32[10,1,512]{2,1,0:T(1,128)}, f32[10,1,512]{2,1,0:T(1,128)S(1)}, u32[]{:S(2)}, u32[]{:S(2)}) collective-permute-start(f32[10,1,512]{2,1,0:T(1,128)} %get-tuple-element.2), channel_id=1, source_target_pairs={{1,0},{3,2},{5,4},{7,6},{9,8},{11,10},{13,12},{15,14},{17,16},{19,... | collective-permute-start | bytes 61448 | tf_op jit(solution)/shard_map/ppermute | solution.py:18
  327.4 110.6 %collective-permute-start.21 = (f32[10,1,512]{2,1,0:T(1,128)}, f32[10,1,512]{2,1,0:T(1,128)S(1)}, u32[]{:S(2)}, u32[]{:S(2)}) collective-permute-start(f32[10,1,512]{2,1,0:T(1,128)} %get-tuple-element.3), channel_id=1, source_target_pairs={{0,1},{2,3},{4,5},{6,7},{8,9},{10,11},{12,13},{14,15},{16,17},{18,... | collective-permute-start | bytes 61448 | tf_op jit(solution)/shard_map/ppermute | solution.py:15
  (9 other events, 503.6 us)
Sparse Core Ops, SparseCore 0:
  178.8 126.4 all-gather.3
  316.4 113.0 all-reduce.5
where the time goes:
time: 450 us; the launch traced here: 449 us
  waiting for transfers between devices  223 us (50%)
  starting transfers between devices  111 us (25%)
  blocking collectives  42.8 us (10%)
  local copies, waits for them, and re-layouts  30.8 us (7%)
  other arithmetic  16.1 us (4%)
  between operations  15.2 us (3%)
  matrix products  9.88 us (2%)
    all_gather x1, waiting for transfers between devices, body(): piece = lax.all_gather(block_traces[None], ('gx', 'gz'), axis=0, tiled=True)  110 us
    psum x1, waiting for transfers between devices, body(): total = lax.psum(partial_rows, 'gy')  99 us
    ppermute x12, starting transfers between devices, extended(): lax.ppermute(lax.slice_in_dim(block, block.shape[dim] - width, None, axis...  64.3 us
    ppermute x12, starting transfers between devices, extended(): lax.ppermute(lax.slice_in_dim(block, 0, width, axis=dim), axis, backward)  46.6 us
    all_gather x1, blocking collectives, body(): face_block = lax.all_gather(face_local, 'gy', axis=1, tiled=True)  42.8 us
    ppermute x12, waiting for transfers between devices, extended(): lax.ppermute(lax.slice_in_dim(block, block.shape[dim] - width, None, axis...  14.4 us
    div x4, other arithmetic, sweep(): return (rhs + beside) / diag  11.1 us
  transfers between devices with their start and end apart: 26, of which 6 were waited for; matrix products, arithmetic and copies ran while one was open for 9% of the time, Pallas kernels for 0%

commit v1 on v0

v1 whole, which is shorter than its diff:
```python
import functools

import jax
import jax.numpy as jnp
from jax import lax
from jax.experimental import pallas as pl
from jax.experimental.pallas import tpu as pltpu
from jax.sharding import PartitionSpec as P

E = 32
CX = 8
YC = 16
DZ = 32
W = YC * E
L = 128
F32 = jnp.float32
BF16 = jnp.bfloat16
I32 = jnp.int32
MESH = pl.DeviceIdType.MESH
HIGHEST = lax.Precision.HIGHEST


def dot_nt(a, b):
    return lax.dot_general(a, b, (((1,), (1,)), ((), ())), preferred_element_type=F32)


def dot_tn(a, b):
    return lax.dot_general(a, b, (((0,), (0,)), ((), ())), preferred_element_type=F32)


def dot_nn(a, b):
    return lax.dot_general(a, b, (((1,), (0,)), ((), ())), preferred_element_type=F32)


def iota(shape, dim):
    return lax.broadcasted_iota(I32, shape, dim)


def along_x(field, low, high):
    rows = iota(field.shape, 0)
    before = jnp.where(rows == 0, low, pltpu.roll(field, 1, 0))
    after = jnp.where(rows == field.shape[0] - 1, high, pltpu.roll(field, field.shape[0] - 1, 0))
    return before + after


def along_y(field, low, high):
    n = field.shape[0]
    lanes = iota((n, L), 1)
    before = pltpu.roll(field, E, 1)
    after = pltpu.roll(field, W - E, 1)
    first = jnp.where(lanes < E, low, before[:, :L])
    last = jnp.where(lanes >= L - E, high, after[:, W - L :])
    before = jnp.concatenate([first, before[:, L:]], axis=1)
    after = jnp.concatenate([after[:, : W - L], last], axis=1)
    return before + after


def kernel(
    cfg,
    ncol, fcol, src, coef, ft, near_h, u_h, v_h,
    sol, flux,
    u1, u2, u3, rinv, planes,
    xs, xr, ys, yr, cr,
    vys, vyr, vzs, vzr,
    ftr, cols_v, cols_s,
    pick, mask, faces, gath,
    near_v, near_p, onehot, u_v, u_p,
    vparts, vblk, tsel, ns, nr, ws, wr, rs, rr,
    load_sem, x_ss, x_rs, c_ss, c_rs, v_ss, v_rs, ft_sem, col_ss, col_rs, smem_sem,
    f_ss, f_rs, g_ss, g_rs, k_ss, k_rs, vp_ss, vp_rs, n_ss, n_rs, w_ss, w_rs, r_ss, r_rs,
):
    n_gx, n_gy, far, rank, total_y = cfg
    tile = CX * total_y
    nq = n_gx // 2
    ring = 2 * n_gy
    gx = lax.axis_index("gx")
    gy = lax.axis_index("gy")
    gz = lax.axis_index("gz")
    zh = lax.rem(gx, 2)
    q = lax.div(gx, 2)
    anti = gx + 1 - 2 * zh
    other = 1 - gz
    me = zh * n_gy + gy
    low_x, high_x = gx > 0, gx < n_gx - 1
    low_y, high_y = gy > 0, gy < n_gy - 1

    def remote(a, b, ssem, rsem, dev):
        return pltpu.make_async_remote_copy(
            src_ref=a, dst_ref=b, send_sem=ssem, recv_sem=rsem, device_id=dev, device_id_type=MESH
        )

    bar = pltpu.get_barrier_semaphore()

    def signal(x, y, z):
        pl.semaphore_signal(bar, inc=1, device_id=(x, y, z), device_id_type=MESH)

    count = ring - 1 + nq - 1 + 1
    for dx, hx in ((-1, low_x), (1, high_x)):
        for dy, hy in ((-1, low_y), (0, None), (1, high_y)):
            cond = hx if hy is None else jnp.logical_and(hx, hy)
            count = count + cond.astype(I32)

            @pl.when(cond)
            def _(dx=dx, dy=dy):
                signal(gx + dx, gy + dy, gz)

    def ring_pos(d):
        pos = lax.rem(me + d, ring)
        return lax.div(pos, n_gy), lax.rem(pos, n_gy)

    def ring_signal(d, c):
        bz, by = ring_pos(d)
        signal(2 * q + bz, by, gz)
        return c

    lax.fori_loop(1, ring, ring_signal, 0)

    def xy_signal(d, c):
        signal(2 * lax.rem(q + d, nq) + zh, gy, gz)
        return c

    lax.fori_loop(1, nq, xy_signal, 0)
    signal(gx, gy, other)

    near_load = pltpu.make_async_copy(near_h, near_v, load_sem.at[0])
    u_load = pltpu.make_async_copy(u_h, u_v, load_sem.at[1])
    v_load = pltpu.make_async_copy(
        v_h.at[:, :, pl.ds(pl.multiple_of(gy * L, L), L)], vparts.at[gy], load_sem.at[2]
    )
    near_load.start()
    u_load.start()
    v_load.start()

    spread = (iota((YC, W), 0) == lax.div(iota((YC, W), 1), E)).astype(F32)

    def first(x, c):
        wide = jnp.dot(coef[x], spread, precision=HIGHEST, preferred_element_type=F32)
        r = 1.0 / (6.0 + wide)
        rinv[x] = r
        u1[x + 1] = src[x] * r
        return c

    lax.fori_loop(0, CX, first, 0)

    rows8 = iota((CX, W), 0)

    def plane(ref, off, depth):
        out = jnp.zeros((CX, W), F32)
        for x in range(CX):
            row = jnp.where(
                gz == 0,
                ref[x + off, depth : depth + 1, :],
                ref[x + off, DZ - 1 - depth : DZ - depth, :],
            )
            out = jnp.where(rows8 == x, row, out)
        return out

    for n, (ref, off, depth) in enumerate(
        ((src, 0, 0), (rinv, 0, 0), (u1, 1, 1), (u1, 1, 0), (src, 0, 1), (rinv, 0, 1), (u1, 1, 2))
    ):
        planes[n] = plane(ref, off, depth)
    for side, (edge, inner, lane) in enumerate(((0, 1, 0), (CX - 1, CX - 2, W - L))):
        for n in range(3):
            xs[side, n : n + 1, :] = planes[n, edge : edge + 1, :]
        xs[side, 3:4, :] = planes[3, inner : inner + 1, :]
        for n in range(4):
            ys[side, n] = planes[n, :, lane : lane + L]

    lanes_col = iota((8, L), 1)
    row = jnp.where(lanes_col == 0, ncol[0], 0)
    for k in range(far):
        row = jnp.where(lanes_col == k + 1, fcol[k], row)
    cols_v[gy] = row

    lanes32 = lax.div(iota((DZ, L), 1), E)

    def pack(u, n):
        def step(k, c):
            low = jnp.zeros((DZ, L), F32)
            high = jnp.zeros((DZ, L), F32)
            for j in range(4):
                cell = u[4 * k + j + 1]
                low = jnp.where(lanes32 == j, pltpu.roll(cell[:, :L], E * j, 1), low)
                high = jnp.where(
                    lanes32 == j, pltpu.roll(cell[:, W - L :], (E * j - (L - E)) % L, 1), high
                )
            vys[n, 0, k] = low
            vys[n, 1, k] = high
            return c

        lax.fori_loop(0, CX // 4, step, 0)

        def zstep(x, c):
            vzs[n, x] = jnp.where(gz == 0, u[x + 1, DZ - 1 : DZ, :], u[x + 1, 0:1, :])
            return c

        lax.fori_loop(0, CX, zstep, 0)

    pack(u1, 0)

    for side, have in ((0, low_x), (1, high_x)):

        @pl.when(jnp.logical_not(have))
        def _(side=side):
            xr[side] = jnp.zeros((4, W), F32)
            for u in (u1, u2, u3):
                u[side * (CX + 1)] = jnp.zeros((DZ, W), F32)

    for side, have in ((0, low_y), (1, high_y)):

        @pl.when(jnp.logical_not(have))
        def _(side=side):
            yr[side] = jnp.zeros((4, CX, L), F32)
            for n in range(3):
                vyr[n, side] = jnp.zeros((CX // 4, DZ, L), F32)

    for a, hx in ((0, low_x), (1, high_x)):
        for b, hy in ((0, low_y), (1, high_y)):

            @pl.when(jnp.logical_not(jnp.logical_and(hx, hy)))
            def _(a=a, b=b):
                cr[2 * a + b] = jnp.zeros((CX, L), F32)

    pl.semaphore_wait(bar, count)

    sides = ((0, low_x, -1), (1, high_x, 1))
    sides_y = ((0, low_y, -1), (1, high_y, 1))

    def x_copy(side, dx):
        return remote(xs.at[side], xr.at[1 - side], x_ss.at[side], x_rs.at[1 - side], (gx + dx, gy, gz))

    def y_copy(side, dy):
        return remote(
            ys.at[side], yr.at[1 - side], x_ss.at[2 + side], x_rs.at[3 - side], (gx, gy + dy, gz)
        )

    def c_copy(a, dx, b, dy):
        there = 2 * (1 - a) + 1 - b
        return remote(
            ys.at[b, 3], cr.at[there], c_ss.at[2 * a + b], c_rs.at[there], (gx + dx, gy + dy, gz)
        )

    def x_halo(act):
        for side, have, dx in sides:

            @pl.when(have)
            def _(side=side, dx=dx):
                act(x_copy(side, dx), 0)

    def c_halo(act):
        for a, hx, dx in sides:
            for b, hy, dy in sides_y:

                @pl.when(jnp.logical_and(hx, hy))
                def _(a=a, dx=dx, b=b, dy=dy):
                    act(c_copy(a, dx, b, dy), 0)

    def y_halo(act):
        for side, have, dy in sides_y:

            @pl.when(have)
            def _(side=side, dy=dy):
                act(y_copy(side, dy), 0)

    def narrow_recv():
        for side, have, dx in sides:

            @pl.when(have)
            def _(side=side, dx=dx):
                remote(
                    xs.at[side], xr.at[side], x_ss.at[side], x_rs.at[side], (gx + dx, gy, gz)
                ).wait_recv()

        for side, have, dy in sides_y:

            @pl.when(have)
            def _(side=side, dy=dy):
                remote(
                    ys.at[side], yr.at[side], x_ss.at[2 + side], x_rs.at[2 + side], (gx, gy + dy, gz)
                ).wait_recv()

        for a, hx, dx in sides:
            for b, hy, dy in sides_y:

                @pl.when(jnp.logical_and(hx, hy))
                def _(a=a, dx=dx, b=b, dy=dy):
                    remote(
                        ys.at[b, 3], cr.at[2 * a + b], c_ss.at[2 * a + b], c_rs.at[2 * a + b],
                        (gx + dx, gy + dy, gz),
                    ).wait_recv()

    def start(copy, _):
        copy.start()

    def sent(copy, _):
        copy.wait_send()

    x_halo(start)
    c_halo(start)
    y_halo(start)

    def ft_copy():
        return remote(ft, ftr, ft_sem.at[0], ft_sem.at[1], (anti, gy, gz))

    ft_copy().start()

    def peer(d):
        return lax.rem(gy + d, n_gy)

    def source_of(d):
        return lax.rem(gy + n_gy - d, n_gy)

    def col_send(d):
        return remote(cols_v.at[gy], cols_v.at[gy], col_ss.at[d], col_rs.at[d], (gx, peer(d), gz))

    def col_recv(d):
        s = source_of(d)
        return remote(cols_v.at[s], cols_v.at[s], col_ss.at[d], col_rs.at[d], (gx, s, gz))

    def vp_send(d):
        t = peer(d)
        return remote(
            v_h.at[:, :, pl.ds(pl.multiple_of(t * L, L), L)], vparts.at[gy],
            vp_ss.at[d], vp_rs.at[d], (gx, t, gz),
        )

    def vp_recv(d):
        s = source_of(d)
        return remote(vparts.at[s], vparts.at[s], vp_ss.at[d], vp_rs.at[d], (gx, s, gz))

    def each(n, f):
        def step(d, c):
            f(d)
            return c

        lax.fori_loop(1, n, step, 0)

    each(n_gy, lambda d: col_send(d).start())

    fields = (u1, u2, u3)

    def vol_send(n, act):
        u = fields[n]
        for side, have, dx in sides:

            @pl.when(have)
            def _(side=side, dx=dx):
                act(
                    remote(
                        u.at[1 + side * (CX - 1)], u.at[(1 - side) * (CX + 1)],
                        v_ss.at[n, side], v_rs.at[n, 1 - side], (gx + dx, gy, gz),
                    ),
                    0,
                )

        for side, have, dy in sides_y:

            @pl.when(have)
            def _(side=side, dy=dy):
                act(
                    remote(
                        vys.at[n, side], vyr.at[n, 1 - side],
                        v_ss.at[n, 2 + side], v_rs.at[n, 3 - side], (gx, gy + dy, gz),
                    ),
                    0,
                )

        act(remote(vzs.at[n], vzr.at[n], v_ss.at[n, 4], v_rs.at[n, 4], (gx, gy, other)), 0)

    def vol_recv(n):
        u = fields[n]
        for side, have, dx in sides:

            @pl.when(have)
            def _(side=side, dx=dx):
                halo = u.at[side * (CX + 1)]
                remote(halo, halo, v_ss.at[n, side], v_rs.at[n, side], (gx + dx, gy, gz)).wait_recv()

        for side, have, dy in sides_y:

            @pl.when(have)
            def _(side=side, dy=dy):
                halo = vyr.at[n, side]
                remote(
                    halo, halo, v_ss.at[n, 2 + side], v_rs.at[n, 2 + side], (gx, gy + dy, gz)
                ).wait_recv()

        remote(vzr.at[n], vzr.at[n], v_ss.at[n, 4], v_rs.at[n, 4], (gx, gy, other)).wait_recv()

    vol_send(0, start)
    each(n_gy, lambda d: vp_send(d).start())

    def tables(table, slot):
        spot = iota((L, total_y), 0) + gy * L
        col = iota((L, total_y), 1)
        cell = jnp.zeros((L, total_y), I32)
        for x in range(CX):
            cell = jnp.where(table[x] == spot, col + x * total_y, cell)
        cell = jnp.sum(cell.astype(F32), axis=1, keepdims=True).astype(I32)
        x = lax.div(cell, total_y)
        y = cell - x * total_y
        y8 = lax.div(y, 8)
        pick[slot] = (iota((L, 16 * n_gy), 1) == y8 * 8 + x).astype(BF16)
        mask[slot] = (lax.div(iota((L, 256), 1), E) == y - y8 * 8).astype(BF16)

    tables(ft, 0)
    spots = iota((tile, L), 0)
    for j in range(n_gy):
        line = jnp.concatenate([ft[x][:, YC * j : YC * (j + 1)] for x in range(CX)], axis=1)
        onehot[:, L * j : L * (j + 1)] = (spots == line).astype(F32).astype(BF16)

    narrow_recv()
    s0, r0, a1, a0 = planes[0], planes[1], planes[2], planes[3]
    s1, r1, a2 = planes[4], planes[5], planes[6]
    lo, hi = yr[0], yr[1]

    def bc(v, n=W):
        return jnp.broadcast_to(v, (CX, n))

    def left(v):
        return pltpu.roll(v, E, 1)

    def right(v):
        return pltpu.roll(v, L - E, 1)

    cor = [[cr[0][CX - 1 :, :], cr[1][CX - 1 :, :]], [cr[2][:1, :], cr[3][:1, :]]]
    edge_u1 = []
    edge_u2 = []
    edge_b1 = []
    for side in range(2):
        hs, hr, h1, h2 = (bc(xr[side, n : n + 1, :]) for n in range(4))
        hu = hs * hr
        at = bc(a0[(CX - 1) * side : (CX - 1) * side + 1, :])
        beside = along_y(hu, left(bc(cor[side][0], L)), right(bc(cor[side][1], L)))
        edge_u1.append(hu)
        edge_b1.append(h1)
        edge_u2.append((hs + h2 + at + h1 + beside) * hr)
    lu2 = lo[0] + left(lo[3]) + right(a0[:, :L]) + lo[2]
    lu2 = (lu2 + along_x(lo[3], bc(cor[0][0], L), bc(cor[1][0], L))) * lo[1]
    hu2 = hi[0] + right(hi[3]) + left(a0[:, W - L :]) + hi[2]
    hu2 = (hu2 + along_x(hi[3], bc(cor[0][1], L), bc(cor[1][1], L))) * hi[1]
    b0 = (s0 + a1 + along_x(a0, edge_u1[0], edge_u1[1]) + along_y(a0, left(lo[3]), right(hi[3]))) * r0
    b1 = (
        s1 + a0 + a2 + along_x(a1, edge_b1[0], edge_b1[1]) + along_y(a1, left(lo[2]), right(hi[2]))
    ) * r1
    face = (s0 + b1 + along_x(b0, edge_u2[0], edge_u2[1]) + along_y(b0, left(lu2), right(hu2))) * r0
    faces[zh, gy] = jnp.concatenate([face[:, : W // 2], face[:, W // 2 :]], axis=0).astype(BF16)

    def ring_d(k):
        half = lax.div(k, 2)
        return n_gy + half * (1 - 2 * lax.rem(k, 2))

    def f_send(k):
        d = ring_d(k)
        bz, by = ring_pos(d)
        return remote(
            faces.at[zh, gy], faces.at[zh, gy], f_ss.at[d], f_rs.at[d], (2 * q + bz, by, gz)
        )

    def f_recv(k):
        d = ring_d(k)
        bz, by = ring_pos(ring - d)
        return remote(
            faces.at[bz, by], faces.at[bz, by], f_ss.at[d], f_rs.at[d], (2 * q + bz, by, gz)
        )

    each(ring, lambda k: f_send(k).start())

    remote(ft, ftr, ft_sem.at[0], ft_sem.at[1], (anti, gy, gz)).wait_recv()
    tables(ftr, 1)
    u_load.wait()
    flat = far * rank
    u_v_all = u_v[...]
    u_p[:flat, :] = dot_nn(u_v_all, onehot[...]).astype(BF16)
    u_p[flat:, :] = jnp.zeros((L - flat, tile), BF16)
    near_load.wait()
    chunk = min(256, tile)
    for n in range(tile // chunk):
        near_p[n * chunk : (n + 1) * chunk, :] = dot_tn(
            near_v[:, n * chunk : (n + 1) * chunk], onehot[...]
        ).astype(BF16)

    rows32 = iota((DZ, W), 0)
    lanes128 = iota((DZ, L), 1)

    def sweep(n, store):
        u = fields[n]

        def step(k, c):
            for j in range(4):
                x = 4 * k + j
                cell = u[x + 1]
                zrow = vzr[n, x]
                up = jnp.where(rows32 == DZ - 1, jnp.where(gz == 0, zrow, 0.0), pltpu.roll(cell, DZ - 1, 0))
                down = jnp.where(rows32 == 0, jnp.where(gz == 0, 0.0, zrow), pltpu.roll(cell, 1, 0))
                low = pltpu.roll(vyr[n, 0, k], (L - E * j) % L, 1)
                high = pltpu.roll(vyr[n, 1, k], (L - E - E * j) % L, 1)
                total = src[x] + u[x] + u[x + 2] + up + down + along_y(cell, low, high)
                store(x, total)
            return c

        lax.fori_loop(0, CX // 4, step, 0)

    def keep(u):
        def store(x, total):
            u[x + 1] = total * rinv[x]

        return store

    each(ring, lambda k: f_recv(k).wait_recv())

    fold = (lax.rem(iota((E, 256), 1), E) == iota((E, 256), 0)).astype(BF16)
    for slot, (half, block) in enumerate(((zh, gx), (1 - zh, anti))):
        flat_faces = faces[half].reshape(16 * n_gy, 256)
        picked = dot_nn(pick[slot], flat_faces).astype(BF16) * mask[slot]
        gath[gz * n_gx + block] = dot_nt(fold, picked).astype(BF16)

    def mine(qq, side):
        return gath.at[pl.ds(side * n_gx + 2 * qq, 2)]

    def g_send(d):
        t = lax.rem(q + d, nq)
        return remote(mine(q, gz), mine(q, gz), g_ss.at[d], g_rs.at[d], (2 * t + zh, gy, gz))

    def g_recv(d):
        s = lax.rem(q + nq - d, nq)
        return remote(mine(s, gz), mine(s, gz), g_ss.at[d], g_rs.at[d], (2 * s + zh, gy, gz))

    def k_send(d):
        s = lax.rem(q + nq - d, nq)
        return remote(mine(s, gz), mine(s, gz), k_ss.at[d], k_rs.at[d], (gx, gy, other))

    def k_recv(d):
        s = lax.rem(q + nq - d, nq)
        return remote(mine(s, other), mine(s, other), k_ss.at[d], k_rs.at[d], (gx, gy, other))

    each(nq, lambda d: g_send(d).start())
    k_send(0).start()

    vol_recv(0)
    sweep(0, keep(u2))
    pack(u2, 1)
    vol_send(1, start)

    v_load.wait()
    each(n_gy, lambda d: vp_recv(d).wait_recv())
    group = lax.div(iota((flat, L), 0), rank)

    def blocks(j, c):
        parts = vparts[j].reshape(flat, L)
        for k in range(far):
            vblk[j, :flat, k * L : (k + 1) * L] = jnp.where(group == k, parts, jnp.zeros_like(parts))
        if flat < L:
            vblk[j, flat:, :] = jnp.zeros((L - flat, far * L), BF16)
        return c

    lax.fori_loop(0, n_gy, blocks, 0)
    each(n_gy, lambda d: col_recv(d).wait_recv())
    to_smem = pltpu.make_async_copy(cols_v, cols_s, smem_sem)
    to_smem.start()
    to_smem.wait()

    def forward(d):
        g_recv(d).wait_recv()
        k_send(d).start()

    each(nq, forward)
    k_recv(0).wait_recv()
    each(nq, lambda d: k_recv(d).wait_recv())

    def w_send(d):
        t = peer(d)
        return remote(ws.at[t], wr.at[gy], w_ss.at[d], w_rs.at[d], (gx, t, gz))

    def w_recv(d):
        s = source_of(d)
        return remote(wr.at[s], wr.at[s], w_ss.at[d], w_rs.at[d], (gx, s, gz))

    def n_send(d):
        t = peer(d)
        return remote(ns.at[t], nr.at[gy], n_ss.at[d], n_rs.at[d], (gx, t, gz))

    def n_recv(d):
        s = source_of(d)
        return remote(nr.at[s], nr.at[s], n_ss.at[d], n_rs.at[d], (gx, s, gz))

    def column(j, k):
        c = cols_s[j, 0, k]
        return gath[lax.rem(c, 2) * n_gx + lax.div(c, 2)]

    def partial_weights(t):
        for k in range(far):
            tsel[:, k * L : (k + 1) * L] = column(t, k + 1)
        return dot_nt(tsel[...], vblk[t])

    def near_out(d):
        t = peer(d)
        ns[t] = column(t, 0)
        n_send(d).start()

    each(n_gy, near_out)
    nr[gy] = column(gy, 0)

    def weights_out(d):
        t = peer(d)
        ws[t] = partial_weights(t)
        w_send(d).start()

    each(n_gy, weights_out)
    wr[gy] = partial_weights(gy)

    vol_recv(1)
    sweep(1, keep(u3))
    pack(u3, 2)
    vol_send(2, start)

    each(n_gy, lambda d: n_recv(d).wait_recv())
    near_t = jnp.concatenate([nr[j] for j in range(n_gy)], axis=1)
    acc = dot_nn(near_t, near_p[...])
    each(n_gy, lambda d: w_recv(d).wait_recv())
    weights = wr[0]
    for j in range(1, n_gy):
        weights = weights + wr[j]
    acc = acc + dot_nn(weights.astype(BF16), u_p[...])
    for j in range(n_gy):
        rs[j] = acc[:, j * L : (j + 1) * L]

    def r_send(d):
        t = peer(d)
        return remote(rs.at[t], rr.at[gy], r_ss.at[d], r_rs.at[d], (gx, t, gz))

    def r_recv(d):
        s = source_of(d)
        return remote(rr.at[s], rr.at[s], r_ss.at[d], r_rs.at[d], (gx, s, gz))

    each(n_gy, lambda d: r_send(d).start())
    rr[gy] = rs[gy]

    def hold(x, total):
        sol[x] = total

    vol_recv(2)
    sweep(2, hold)
    each(n_gy, lambda d: r_recv(d).wait_recv())
    total = rr[0]
    for j in range(1, n_gy):
        total = total + rr[j]
    widen = (iota((E, W), 0) == lax.rem(iota((E, W), 1), E)).astype(F32)
    wide = jnp.dot(total.T, widen, precision=HIGHEST, preferred_element_type=F32)
    keep_cell = lax.rem(iota((L, W), 0), YC) == lax.div(iota((L, W), 1), E)
    value = jnp.sum(jnp.where(keep_cell, wide, 0.0).reshape(CX, YC, W), axis=1)
    face_z = (DZ - 1) * gz
    for x in range(CX):
        line = value[x : x + 1, :]
        flux[x] = line
        sol[x] = (sol[x] + jnp.where(rows32 == face_z, line, 0.0)) * rinv[x]

    x_halo(sent)
    c_halo(sent)
    y_halo(sent)
    ft_copy().wait_send()
    for n in range(3):
        vol_send(n, sent)
    each(n_gy, lambda d: col_send(d).wait_send())
    each(n_gy, lambda d: vp_send(d).wait_send())
    each(ring, lambda k: f_send(k).wait_send())
    each(nq, lambda d: g_send(d).wait_send())
    k_send(0).wait_send()
    each(nq, lambda d: k_send(d).wait_send())
    each(n_gy, lambda d: n_send(d).wait_send())
    each(n_gy, lambda d: w_send(d).wait_send())
    each(n_gy, lambda d: r_send(d).wait_send())


def body(source, coef, face_trace, near_col, far_col, near_tile, far_u, far_v):
    n_gx = lax.axis_size("gx")
    n_gy = lax.axis_size("gy")
    far, rank, tile = far_u.shape[3:]
    total_y = face_trace.shape[2]
    nq, ring, flat = n_gx // 2, 2 * n_gy, far * rank
    cfg = (n_gx, n_gy, far, rank, total_y)
    vmem = pl.BlockSpec(memory_space=pltpu.VMEM)
    smem = pl.BlockSpec(memory_space=pltpu.SMEM)
    anyspace = pl.BlockSpec(memory_space=pl.ANY)
    dma = pltpu.SemaphoreType.DMA
    scratch = [
        pltpu.VMEM((CX + 2, DZ, W), F32),
        pltpu.VMEM((CX + 2, DZ, W), F32),
        pltpu.VMEM((CX + 2, DZ, W), F32),
        pltpu.VMEM((CX, DZ, W), F32),
        pltpu.VMEM((7, CX, W), F32),
        pltpu.VMEM((2, 4, W), F32),
        pltpu.VMEM((2, 4, W), F32),
        pltpu.VMEM((2, 4, CX, L), F32),
        pltpu.VMEM((2, 4, CX, L), F32),
        pltpu.VMEM((4, CX, L), F32),
        pltpu.VMEM((3, 2, CX // 4, DZ, L), F32),
        pltpu.VMEM((3, 2, CX // 4, DZ, L), F32),
        pltpu.VMEM((3, CX, 1, W), F32),
        pltpu.VMEM((3, CX, 1, W), F32),
        pltpu.VMEM((CX, 1, total_y), I32),
        pltpu.VMEM((n_gy, 8, L), I32),
        pltpu.SMEM((n_gy, 8, L), I32),
        pltpu.VMEM((2, L, 16 * n_gy), BF16),
        pltpu.VMEM((2, L, 256), BF16),
        pltpu.VMEM((2, n_gy, 16, 256), BF16),
        pltpu.VMEM((2 * n_gx, E, L), BF16),
        pltpu.VMEM((tile, tile), BF16),
        pltpu.VMEM((tile, tile), BF16),
        pltpu.VMEM((tile, tile), BF16),
        pltpu.VMEM((flat, tile), BF16),
        pltpu.VMEM((L, tile), BF16),
        pltpu.VMEM((n_gy, far, rank, L), BF16),
        pltpu.VMEM((n_gy, L, far * L), BF16),
        pltpu.VMEM((E, far * L), BF16),
        pltpu.VMEM((n_gy, E, L), BF16),
        pltpu.VMEM((n_gy, E, L), BF16),
        pltpu.VMEM((n_gy, E, L), F32),
        pltpu.VMEM((n_gy, E, L), F32),
        pltpu.VMEM((n_gy, E, L), F32),
        pltpu.VMEM((n_gy, E, L), F32),
        dma((3,)),
        dma((4,)), dma((4,)),
        dma((4,)), dma((4,)),
        dma((3, 5)), dma((3, 5)),
        dma((2,)),
        dma((n_gy,)), dma((n_gy,)),
        dma,
        dma((ring,)), dma((ring,)),
        dma((nq,)), dma((nq,)),
        dma((nq,)), dma((nq,)),
        dma((n_gy,)), dma((n_gy,)),
        dma((n_gy,)), dma((n_gy,)),
        dma((n_gy,)), dma((n_gy,)),
        dma((n_gy,)), dma((n_gy,)),
    ]
    return pl.pallas_call(
        functools.partial(kernel, cfg),
        out_shape=(
            jax.ShapeDtypeStruct(source.shape, F32),
            jax.ShapeDtypeStruct((CX, 1, W), F32),
        ),
        in_specs=[smem, smem, vmem, vmem, vmem, anyspace, anyspace, anyspace],
        out_specs=(vmem, vmem),
        scratch_shapes=scratch,
        compiler_params=pltpu.CompilerParams(
            collective_id=0, has_side_effects=True, vmem_limit_bytes=48 * 1024 * 1024
        ),
        name="coupled_step",
    )(
        near_col.reshape(1),
        far_col.reshape(far),
        source,
        coef,
        face_trace,
        near_tile.reshape(tile, tile),
        far_u.reshape(flat, tile),
        far_v.reshape(far, rank, tile),
    )


def solution(mesh):
    return jax.shard_map(
        body,
        mesh=mesh,
        in_specs=(
            P("gx", "gz", "gy"),
            P("gx", "gz", "gy"),
            P("gx", "gz", None),
            P("gx", "gz", "gy"),
            P("gx", "gz", "gy", None),
            P("gx", "gz", "gy", None, None),
            P("gx", "gz", "gy", None, None, None),
            P("gx", "gz", "gy", None, None, None),
        ),
        out_specs=(P("gx", "gz", "gy"), P("gx", "gz", "gy")),
        check_vma=False,
    )
```

time: 450 us -> 108 us (0.24)
  waiting for transfers between devices: 223 us -> 0 us
  starting transfers between devices: 111 us -> 0 us
  Pallas kernels: 0 us -> 98.6 us
  blocking collectives: 42.8 us -> 0 us
  local copies, waits for them, and re-layouts: 30.8 us -> 8.17 us
  other arithmetic: 16.1 us -> 0 us
  between operations: 15.2 us -> 1.31 us
  matrix products: 9.88 us -> 0 us
    ppermute x24 -> x0, starting transfers between devices: 111 us -> none  [the longest x12 64.3 us: extended(): lax.ppermute(lax.slice_in_dim(block, block.shape[dim] - width, None, axis...]
    all_gather x1 -> x0, waiting for transfers between devices: 110 us -> none  [body(): piece = lax.all_gather(block_traces[None], ('gx', 'gz'), axis=0, tiled=True)]
    psum x1 -> x0, waiting for transfers between devices: 99 us -> none  [body(): total = lax.psum(partial_rows, 'gy')]
    pallas_call x0 -> x1, Pallas kernels: none -> 98.6 us  [body(): pl.pallas_call(functools.partial(kernel, cfg), out_shape=(jax.ShapeDtypeS...]
    all_gather x1 -> x0, blocking collectives: 42.8 us -> none  [body(): face_block = lax.all_gather(face_local, 'gy', axis=1, tiled=True)]
    ppermute x24 -> x0, waiting for transfers between devices: 14.4 us -> none  [the longest x12 14.4 us: extended(): lax.ppermute(lax.slice_in_dim(block, block.shape[dim] - width, None, axis...]
    div x4 -> x0, other arithmetic: 11.1 us -> none  [sweep(): return (rhs + beside) / diag]
    dot_general x3 -> x0, matrix products: 9.88 us -> none  [the longest x1 6.66 us: body(): jnp.einsum('cn,net->cet', onehot, piece, preferred_element_type=jnp.float32)]
  transfers between devices with their start and end apart: 26 -> 0, of which waited for: 6 -> 0; matrix products, arithmetic and copies ran while one was open for 9% -> 0% of each run, Pallas kernels for 0% -> 0%
where the time goes in v1:
time: 108 us
  Pallas kernels  98.6 us (91%)
  local copies, waits for them, and re-layouts  8.17 us (8%)
  between operations  1.31 us (1%)
    pallas_call x1, Pallas kernels, body(): pl.pallas_call(functools.partial(kernel, cfg), out_shape=(jax.ShapeDtypeS...  98.6 us
    unnamed x15, local copies, waits for them, and re-layouts  8.17 us

profile of v1, /device:TPU:24, one launch (start us, length us, event | category | flops | bytes accessed | tf_op | source)
XLA Modules:
  0.0 108.1 jit_solution(17931939387824925064)
XLA Ops:
  1.3 0.9 copy.10.coef
  2.2 0.0 copy-start
  2.2 1.6 %copy-done = bf16[1,1,1,1024,1024]{4,3,2,1,0:T(8,128)(2,1)S(1)} copy-done((bf16[1,1,1,1024,1024]{4,3,2,1,0:T(8,128)(2,1)S(1)}, bf16[1,1,1,1024,1024]{4,3,2,1,0:T(8,128)(2,1)}, u32[]{:S(2)}) %copy-start) | copy-done | bytes 2097176
  3.8 0.0 copy-start.1
  3.8 1.0 copy-done.1
  4.9 0.0 copy-start.2
  4.9 0.9 copy-done.2
  5.8 0.0 copy-start.3
  5.8 0.9 copy-done.3
  6.7 0.0 copy-start.4
  6.7 0.7 copy-done.4
  7.4 0.0 copy-start.5
  7.4 0.7 copy-done.5
  8.1 98.6 %coupled_step.1 = (f32[8,32,512]{2,1,0:T(8,128)S(1)}, f32[8,1,512]{2,1,0:T(1,128)S(1)}) custom-call(s32[1]{0:T(128)} %bitcast.5.ncol, s32[7]{0:T(128)S(1)} %bitcast.9, f32[8,32,512]{2,1,0:T(8,128)S(1)} %copy-done.1, f32[8,32,16]{2,1,0:T(8,128)S(1)} %copy.10.coef, s32[8,1,128]{2,1,0:T(1,128)S(1)} %copy-done.4, bf16[1024,1024]{1,0:T(8,128)(2,1)S(1)} %bitcast.6, ...), custom_call_target="tpu_custom_call" | custom-call | tf_op jit(solution)/shard_map/coupled_step/pallas_call | solution.py:737
  106.7 0.8 copy.14
  107.5 0.6 copy.15
Async XLA Ops:
  2.2 1.6 %copy-start = (bf16[1,1,1,1024,1024]{4,3,2,1,0:T(8,128)(2,1)S(1)}, bf16[1,1,1,1024,1024]{4,3,2,1,0:T(8,128)(2,1)}, u32[]{:S(2)}) copy-start(bf16[1,1,1,1024,1024]{4,3,2,1,0:T(8,128)(2,1)} %param.13) | copy-start | bytes 6291460
  3.8 1.0 copy-start.1
  4.9 0.9 copy-start.2
  5.8 0.9 copy-start.3
  6.7 0.7 copy-start.4
  7.4 0.7 copy-start.5

commit v2 on v1

--- a/solution.py
+++ b/solution.py
@@ -16,6 +16,7 @@
 F32 = jnp.float32
 BF16 = jnp.bfloat16
 I32 = jnp.int32
+TEAM = 4
 MESH = pl.DeviceIdType.MESH
 HIGHEST = lax.Precision.HIGHEST
 
@@ -57,20 +58,23 @@
 
 def kernel(
     cfg,
-    ncol, fcol, src, coef, ft, near_h, u_h, v_h,
+    ncol_h, fcol_h, src_h, coef_h, ft_h, near_h, u_h, v_h,
     sol, flux,
+    ncol, fcol, src, coef, ft,
     u1, u2, u3, rinv, planes,
-    xs, xr, ys, yr, cr,
-    vys, vyr, vzs, vzr,
+    xs, xr, ys, yr, cs, cr,
+    vxs, vxr, vys, vyr, vzs, vzr,
     ftr, cols_v, cols_s,
     pick, mask, faces, gath,
     near_v, near_p, onehot, u_v, u_p,
     vparts, vblk, tsel, ns, nr, ws, wr, rs, rr,
-    load_sem, x_ss, x_rs, c_ss, c_rs, v_ss, v_rs, ft_sem, col_ss, col_rs, smem_sem,
+    load_sem, in_sem, x_ss, x_rs, c_ss, c_rs, v_ss, v_rs, ft_sem, col_ss, col_rs, smem_sem,
     f_ss, f_rs, g_ss, g_rs, k_ss, k_rs, vp_ss, vp_rs, n_ss, n_rs, w_ss, w_rs, r_ss, r_rs,
 ):
     n_gx, n_gy, far, rank, total_y = cfg
     tile = CX * total_y
+    team = min(TEAM, n_gy)
+    part = tile // team
     nq = n_gx // 2
     ring = 2 * n_gy
     gx = lax.axis_index("gx")
@@ -81,6 +85,8 @@
     anti = gx + 1 - 2 * zh
     other = 1 - gz
     me = zh * n_gy + gy
+    seat = lax.rem(gy, team)
+    bench = gy - seat
     low_x, high_x = gx > 0, gx < n_gx - 1
     low_y, high_y = gy > 0, gy < n_gy - 1
 
@@ -122,10 +128,18 @@
     lax.fori_loop(1, nq, xy_signal, 0)
     signal(gx, gy, other)
 
+    loads = [
+        pltpu.make_async_copy(a, b, in_sem.at[n])
+        for n, (a, b) in enumerate(
+            ((coef_h, coef), (src_h, src), (ft_h, ft), (ncol_h, ncol), (fcol_h, fcol))
+        )
+    ]
+    for load in loads:
+        load.start()
     near_load = pltpu.make_async_copy(near_h, near_v, load_sem.at[0])
     u_load = pltpu.make_async_copy(u_h, u_v, load_sem.at[1])
     v_load = pltpu.make_async_copy(
-        v_h.at[:, :, pl.ds(pl.multiple_of(gy * L, L), L)], vparts.at[gy], load_sem.at[2]
+        v_h.at[:, :, pl.ds(pl.multiple_of(seat * part, L), part)], vparts.at[seat], load_sem.at[2]
     )
     near_load.start()
     u_load.start()
@@ -134,12 +148,17 @@
     spread = (iota((YC, W), 0) == lax.div(iota((YC, W), 1), E)).astype(F32)
 
     def first(x, c):
-        wide = jnp.dot(coef[x], spread, precision=HIGHEST, preferred_element_type=F32)
+        wide = lax.dot_general(
+            coef[x], spread, (((0,), (0,)), ((), ())),
+            precision=HIGHEST, preferred_element_type=F32,
+        )
         r = 1.0 / (6.0 + wide)
         rinv[x] = r
         u1[x + 1] = src[x] * r
         return c
 
+    for load in loads:
+        load.wait()
     lax.fori_loop(0, CX, first, 0)
 
     rows8 = iota((CX, W), 0)
@@ -165,16 +184,22 @@
         xs[side, 3:4, :] = planes[3, inner : inner + 1, :]
         for n in range(4):
             ys[side, n] = planes[n, :, lane : lane + L]
+        for b, lane_b in enumerate((0, W - L)):
+            cs[2 * side + b] = planes[3, edge : edge + 1, lane_b : lane_b + L]
 
     lanes_col = iota((8, L), 1)
-    row = jnp.where(lanes_col == 0, ncol[0], 0)
+    row = jnp.where(lanes_col == 0, ncol[0, 0, 0], 0)
     for k in range(far):
-        row = jnp.where(lanes_col == k + 1, fcol[k], row)
-    cols_v[gy] = row
+        row = jnp.where(lanes_col == k + 1, fcol[0, 0, 0, k], row)
+    cols_v[seat] = row
 
     lanes32 = lax.div(iota((DZ, L), 1), E)
 
     def pack(u, n):
+        if n == 1:
+            vxs[0] = u[1].astype(BF16)
+            vxs[1] = u[CX].astype(BF16)
+
         def step(k, c):
             low = jnp.zeros((DZ, L), F32)
             high = jnp.zeros((DZ, L), F32)
@@ -219,7 +244,7 @@
 
             @pl.when(jnp.logical_not(jnp.logical_and(hx, hy)))
             def _(a=a, b=b):
-                cr[2 * a + b] = jnp.zeros((CX, L), F32)
+                cr[2 * a + b] = jnp.zeros((1, L), F32)
 
     pl.semaphore_wait(bar, count)
 
@@ -237,7 +262,7 @@
     def c_copy(a, dx, b, dy):
         there = 2 * (1 - a) + 1 - b
         return remote(
-            ys.at[b, 3], cr.at[there], c_ss.at[2 * a + b], c_rs.at[there], (gx + dx, gy + dy, gz)
+            cs.at[2 * a + b], cr.at[there], c_ss.at[2 * a + b], c_rs.at[there], (gx + dx, gy + dy, gz)
         )
 
     def x_halo(act):
@@ -285,7 +310,7 @@
                 @pl.when(jnp.logical_and(hx, hy))
                 def _(a=a, dx=dx, b=b, dy=dy):
                     remote(
-                        ys.at[b, 3], cr.at[2 * a + b], c_ss.at[2 * a + b], c_rs.at[2 * a + b],
+                        cs.at[2 * a + b], cr.at[2 * a + b], c_ss.at[2 * a + b], c_rs.at[2 * a + b],
                         (gx + dx, gy + dy, gz),
                     ).wait_recv()
 
@@ -310,23 +335,31 @@
     def source_of(d):
         return lax.rem(gy + n_gy - d, n_gy)
 
+    def mate(d):
+        return lax.rem(seat + d, team)
+
+    def mate_from(d):
+        return lax.rem(seat + team - d, team)
+
     def col_send(d):
-        return remote(cols_v.at[gy], cols_v.at[gy], col_ss.at[d], col_rs.at[d], (gx, peer(d), gz))
+        return remote(
+            cols_v.at[seat], cols_v.at[seat], col_ss.at[d], col_rs.at[d], (gx, bench + mate(d), gz)
+        )
 
     def col_recv(d):
-        s = source_of(d)
-        return remote(cols_v.at[s], cols_v.at[s], col_ss.at[d], col_rs.at[d], (gx, s, gz))
+        s = mate_from(d)
+        return remote(cols_v.at[s], cols_v.at[s], col_ss.at[d], col_rs.at[d], (gx, bench + s, gz))
 
     def vp_send(d):
-        t = peer(d)
+        t = mate(d)
         return remote(
-            v_h.at[:, :, pl.ds(pl.multiple_of(t * L, L), L)], vparts.at[gy],
-            vp_ss.at[d], vp_rs.at[d], (gx, t, gz),
+            v_h.at[:, :, pl.ds(pl.multiple_of(t * part, L), part)], vparts.at[seat],
+            vp_ss.at[d], vp_rs.at[d], (gx, bench + t, gz),
         )
 
     def vp_recv(d):
-        s = source_of(d)
-        return remote(vparts.at[s], vparts.at[s], vp_ss.at[d], vp_rs.at[d], (gx, s, gz))
+        s = mate_from(d)
+        return remote(vparts.at[s], vparts.at[s], vp_ss.at[d], vp_rs.at[d], (gx, bench + s, gz))
 
     def each(n, f):
         def step(d, c):
@@ -335,7 +368,7 @@
 
         lax.fori_loop(1, n, step, 0)
 
-    each(n_gy, lambda d: col_send(d).start())
+    each(team, lambda d: col_send(d).start())
 
     fields = (u1, u2, u3)
 
@@ -345,9 +378,11 @@
 
             @pl.when(have)
             def _(side=side, dx=dx):
+                out = vxs.at[side] if n == 1 else u.at[1 + side * (CX - 1)]
+                there = vxr.at[1 - side] if n == 1 else u.at[(1 - side) * (CX + 1)]
                 act(
                     remote(
-                        u.at[1 + side * (CX - 1)], u.at[(1 - side) * (CX + 1)],
+                        out, there,
                         v_ss.at[n, side], v_rs.at[n, 1 - side], (gx + dx, gy, gz),
                     ),
                     0,
@@ -373,8 +408,10 @@
 
             @pl.when(have)
             def _(side=side, dx=dx):
-                halo = u.at[side * (CX + 1)]
+                halo = vxr.at[side] if n == 1 else u.at[side * (CX + 1)]
                 remote(halo, halo, v_ss.at[n, side], v_rs.at[n, side], (gx + dx, gy, gz)).wait_recv()
+                if n == 1:
+                    u[side * (CX + 1)] = vxr[side].astype(F32)
 
         for side, have, dy in sides_y:
 
@@ -388,20 +425,19 @@
         remote(vzr.at[n], vzr.at[n], v_ss.at[n, 4], v_rs.at[n, 4], (gx, gy, other)).wait_recv()
 
     vol_send(0, start)
-    each(n_gy, lambda d: vp_send(d).start())
 
     def tables(table, slot):
-        spot = iota((L, total_y), 0) + gy * L
-        col = iota((L, total_y), 1)
-        cell = jnp.zeros((L, total_y), I32)
+        spot = iota((part, total_y), 0) + seat * part
+        col = iota((part, total_y), 1)
+        cell = jnp.zeros((part, total_y), I32)
         for x in range(CX):
             cell = jnp.where(table[x] == spot, col + x * total_y, cell)
         cell = jnp.sum(cell.astype(F32), axis=1, keepdims=True).astype(I32)
         x = lax.div(cell, total_y)
         y = cell - x * total_y
         y8 = lax.div(y, 8)
-        pick[slot] = (iota((L, 16 * n_gy), 1) == y8 * 8 + x).astype(BF16)
-        mask[slot] = (lax.div(iota((L, 256), 1), E) == y - y8 * 8).astype(BF16)
+        pick[slot] = (iota((part, 16 * n_gy), 1) == y8 * 8 + x).astype(BF16)
+        mask[slot] = (lax.div(iota((part, 256), 1), E) == y - y8 * 8).astype(BF16)
 
     tables(ft, 0)
     spots = iota((tile, L), 0)
@@ -423,7 +459,7 @@
     def right(v):
         return pltpu.roll(v, L - E, 1)
 
-    cor = [[cr[0][CX - 1 :, :], cr[1][CX - 1 :, :]], [cr[2][:1, :], cr[3][:1, :]]]
+    cor = [[cr[0], cr[1]], [cr[2], cr[3]]]
     edge_u1 = []
     edge_u2 = []
     edge_b1 = []
@@ -466,6 +502,8 @@
 
     each(ring, lambda k: f_send(k).start())
 
+    each(team, lambda d: vp_send(d).start())
+
     remote(ft, ftr, ft_sem.at[0], ft_sem.at[1], (anti, gy, gz)).wait_recv()
     tables(ftr, 1)
     u_load.wait()
@@ -507,6 +545,11 @@
 
         return store
 
+    each(team, lambda d: col_recv(d).wait_recv())
+    to_smem = pltpu.make_async_copy(cols_v, cols_s, smem_sem)
+    to_smem.start()
+    to_smem.wait()
+
     each(ring, lambda k: f_recv(k).wait_recv())
 
     fold = (lax.rem(iota((E, 256), 1), E) == iota((E, 256), 0)).astype(BF16)
@@ -543,22 +586,18 @@
     vol_send(1, start)
 
     v_load.wait()
-    each(n_gy, lambda d: vp_recv(d).wait_recv())
-    group = lax.div(iota((flat, L), 0), rank)
+    each(team, lambda d: vp_recv(d).wait_recv())
+    group = lax.div(iota((flat, part), 0), rank)
 
     def blocks(j, c):
-        parts = vparts[j].reshape(flat, L)
+        parts = vparts[j].reshape(flat, part)
         for k in range(far):
-            vblk[j, :flat, k * L : (k + 1) * L] = jnp.where(group == k, parts, jnp.zeros_like(parts))
+            vblk[j, :flat, k * part : (k + 1) * part] = jnp.where(group == k, parts, jnp.zeros_like(parts))
         if flat < L:
-            vblk[j, flat:, :] = jnp.zeros((L - flat, far * L), BF16)
+            vblk[j, flat:, :] = jnp.zeros((L - flat, far * part), BF16)
         return c
 
-    lax.fori_loop(0, n_gy, blocks, 0)
-    each(n_gy, lambda d: col_recv(d).wait_recv())
-    to_smem = pltpu.make_async_copy(cols_v, cols_s, smem_sem)
-    to_smem.start()
-    to_smem.wait()
+    lax.fori_loop(0, team, blocks, 0)
 
     def forward(d):
         g_recv(d).wait_recv()
@@ -569,20 +608,20 @@
     each(nq, lambda d: k_recv(d).wait_recv())
 
     def w_send(d):
-        t = peer(d)
-        return remote(ws.at[t], wr.at[gy], w_ss.at[d], w_rs.at[d], (gx, t, gz))
+        t = mate(d)
+        return remote(ws.at[t], wr.at[seat], w_ss.at[d], w_rs.at[d], (gx, bench + t, gz))
 
     def w_recv(d):
-        s = source_of(d)
-        return remote(wr.at[s], wr.at[s], w_ss.at[d], w_rs.at[d], (gx, s, gz))
+        s = mate_from(d)
+        return remote(wr.at[s], wr.at[s], w_ss.at[d], w_rs.at[d], (gx, bench + s, gz))
 
     def n_send(d):
-        t = peer(d)
-        return remote(ns.at[t], nr.at[gy], n_ss.at[d], n_rs.at[d], (gx, t, gz))
+        t = mate(d)
+        return remote(ns.at[t], nr.at[seat], n_ss.at[d], n_rs.at[d], (gx, bench + t, gz))
 
     def n_recv(d):
-        s = source_of(d)
-        return remote(nr.at[s], nr.at[s], n_ss.at[d], n_rs.at[d], (gx, s, gz))
+        s = mate_from(d)
+        return remote(nr.at[s], nr.at[s], n_ss.at[d], n_rs.at[d], (gx, bench + s, gz))
 
     def column(j, k):
         c = cols_s[j, 0, k]
@@ -590,36 +629,36 @@
 
     def partial_weights(t):
         for k in range(far):
-            tsel[:, k * L : (k + 1) * L] = column(t, k + 1)
+            tsel[:, k * part : (k + 1) * part] = column(t, k + 1)
         return dot_nt(tsel[...], vblk[t])
 
     def near_out(d):
-        t = peer(d)
+        t = mate(d)
         ns[t] = column(t, 0)
         n_send(d).start()
 
-    each(n_gy, near_out)
-    nr[gy] = column(gy, 0)
+    each(team, near_out)
+    nr[seat] = column(seat, 0)
 
     def weights_out(d):
-        t = peer(d)
+        t = mate(d)
         ws[t] = partial_weights(t)
         w_send(d).start()
 
-    each(n_gy, weights_out)
-    wr[gy] = partial_weights(gy)
+    each(team, weights_out)
+    wr[seat] = partial_weights(seat)
 
     vol_recv(1)
     sweep(1, keep(u3))
     pack(u3, 2)
     vol_send(2, start)
 
-    each(n_gy, lambda d: n_recv(d).wait_recv())
-    near_t = jnp.concatenate([nr[j] for j in range(n_gy)], axis=1)
+    each(team, lambda d: n_recv(d).wait_recv())
+    near_t = jnp.concatenate([nr[j] for j in range(team)], axis=1)
     acc = dot_nn(near_t, near_p[...])
-    each(n_gy, lambda d: w_recv(d).wait_recv())
+    each(team, lambda d: w_recv(d).wait_recv())
     weights = wr[0]
-    for j in range(1, n_gy):
+    for j in range(1, team):
         weights = weights + wr[j]
     acc = acc + dot_nn(weights.astype(BF16), u_p[...])
     for j in range(n_gy):
@@ -639,6 +678,20 @@
     def hold(x, total):
         sol[x] = total
 
+    x_halo(sent)
+    c_halo(sent)
+    y_halo(sent)
+    ft_copy().wait_send()
+    each(team, lambda d: col_send(d).wait_send())
+    each(team, lambda d: vp_send(d).wait_send())
+    each(ring, lambda k: f_send(k).wait_send())
+    each(nq, lambda d: g_send(d).wait_send())
+    k_send(0).wait_send()
+    each(nq, lambda d: k_send(d).wait_send())
+    each(team, lambda d: n_send(d).wait_send())
+    each(team, lambda d: w_send(d).wait_send())
+    for n in range(3):
+        vol_send(n, sent)
     vol_recv(2)
     sweep(2, hold)
     each(n_gy, lambda d: r_recv(d).wait_recv())
@@ -655,20 +708,6 @@
         flux[x] = line
         sol[x] = (sol[x] + jnp.where(rows32 == face_z, line, 0.0)) * rinv[x]
 
-    x_halo(sent)
-    c_halo(sent)
-    y_halo(sent)
-    ft_copy().wait_send()
-    for n in range(3):
-        vol_send(n, sent)
-    each(n_gy, lambda d: col_send(d).wait_send())
-    each(n_gy, lambda d: vp_send(d).wait_send())
-    each(ring, lambda k: f_send(k).wait_send())
-    each(nq, lambda d: g_send(d).wait_send())
-    k_send(0).wait_send()
-    each(nq, lambda d: k_send(d).wait_send())
-    each(n_gy, lambda d: n_send(d).wait_send())
-    each(n_gy, lambda d: w_send(d).wait_send())
     each(n_gy, lambda d: r_send(d).wait_send())
 
 
@@ -678,12 +717,18 @@
     far, rank, tile = far_u.shape[3:]
     total_y = face_trace.shape[2]
     nq, ring, flat = n_gx // 2, 2 * n_gy, far * rank
+    team = min(TEAM, n_gy)
+    part = tile // team
     cfg = (n_gx, n_gy, far, rank, total_y)
     vmem = pl.BlockSpec(memory_space=pltpu.VMEM)
-    smem = pl.BlockSpec(memory_space=pltpu.SMEM)
     anyspace = pl.BlockSpec(memory_space=pl.ANY)
     dma = pltpu.SemaphoreType.DMA
     scratch = [
+        pltpu.SMEM((1, 1, 1), I32),
+        pltpu.SMEM((1, 1, 1, far), I32),
+        pltpu.VMEM((CX, DZ, W), F32),
+        pltpu.VMEM((CX, YC, DZ), F32),
+        pltpu.VMEM((CX, 1, total_y), I32),
         pltpu.VMEM((CX + 2, DZ, W), F32),
         pltpu.VMEM((CX + 2, DZ, W), F32),
         pltpu.VMEM((CX + 2, DZ, W), F32),
@@ -693,33 +738,37 @@
         pltpu.VMEM((2, 4, W), F32),
         pltpu.VMEM((2, 4, CX, L), F32),
         pltpu.VMEM((2, 4, CX, L), F32),
-        pltpu.VMEM((4, CX, L), F32),
+        pltpu.VMEM((4, 1, L), F32),
+        pltpu.VMEM((4, 1, L), F32),
+        pltpu.VMEM((2, DZ, W), BF16),
+        pltpu.VMEM((2, DZ, W), BF16),
         pltpu.VMEM((3, 2, CX // 4, DZ, L), F32),
         pltpu.VMEM((3, 2, CX // 4, DZ, L), F32),
         pltpu.VMEM((3, CX, 1, W), F32),
         pltpu.VMEM((3, CX, 1, W), F32),
         pltpu.VMEM((CX, 1, total_y), I32),
-        pltpu.VMEM((n_gy, 8, L), I32),
-        pltpu.SMEM((n_gy, 8, L), I32),
-        pltpu.VMEM((2, L, 16 * n_gy), BF16),
-        pltpu.VMEM((2, L, 256), BF16),
+        pltpu.VMEM((team, 8, L), I32),
+        pltpu.SMEM((team, 8, L), I32),
+        pltpu.VMEM((2, part, 16 * n_gy), BF16),
+        pltpu.VMEM((2, part, 256), BF16),
         pltpu.VMEM((2, n_gy, 16, 256), BF16),
-        pltpu.VMEM((2 * n_gx, E, L), BF16),
+        pltpu.VMEM((2 * n_gx, E, part), BF16),
         pltpu.VMEM((tile, tile), BF16),
         pltpu.VMEM((tile, tile), BF16),
         pltpu.VMEM((tile, tile), BF16),
         pltpu.VMEM((flat, tile), BF16),
         pltpu.VMEM((L, tile), BF16),
-        pltpu.VMEM((n_gy, far, rank, L), BF16),
-        pltpu.VMEM((n_gy, L, far * L), BF16),
-        pltpu.VMEM((E, far * L), BF16),
-        pltpu.VMEM((n_gy, E, L), BF16),
-        pltpu.VMEM((n_gy, E, L), BF16),
-        pltpu.VMEM((n_gy, E, L), F32),
-        pltpu.VMEM((n_gy, E, L), F32),
+        pltpu.VMEM((team, far, rank, part), BF16),
+        pltpu.VMEM((team, L, far * part), BF16),
+        pltpu.VMEM((E, far * part), BF16),
+        pltpu.VMEM((team, E, part), BF16),
+        pltpu.VMEM((team, E, part), BF16),
+        pltpu.VMEM((team, E, L), F32),
+        pltpu.VMEM((team, E, L), F32),
         pltpu.VMEM((n_gy, E, L), F32),
         pltpu.VMEM((n_gy, E, L), F32),
         dma((3,)),
+        dma((5,)),
         dma((4,)), dma((4,)),
         dma((4,)), dma((4,)),
         dma((3, 5)), dma((3, 5)),
@@ -740,18 +789,18 @@
             jax.ShapeDtypeStruct(source.shape, F32),
             jax.ShapeDtypeStruct((CX, 1, W), F32),
         ),
-        in_specs=[smem, smem, vmem, vmem, vmem, anyspace, anyspace, anyspace],
+        in_specs=[anyspace] * 8,
         out_specs=(vmem, vmem),
         scratch_shapes=scratch,
         compiler_params=pltpu.CompilerParams(
-            collective_id=0, has_side_effects=True, vmem_limit_bytes=48 * 1024 * 1024
+            collective_id=0, has_side_effects=True, vmem_limit_bytes=60 * 1024 * 1024
         ),
         name="coupled_step",
     )(
-        near_col.reshape(1),
-        far_col.reshape(far),
+        near_col,
+        far_col,
         source,
-        coef,
+        coef.swapaxes(1, 2),
         face_trace,
         near_tile.reshape(tile, tile),
         far_u.reshape(flat, tile),

time: 108 us -> 81.1 us (0.75)
  the two profiles are of different devices: /device:TPU:24 before, /device:TPU:73 now
where the time goes in v2:
time: 81.1 us; the launch traced here: 80.8 us
  Pallas kernels  76.3 us (94%)
  local copies, waits for them, and re-layouts  3.19 us (4%)
  between operations  1.29 us (2%)
    pallas_call x1, Pallas kernels, body(): pl.pallas_call(functools.partial(kernel, cfg), out_shape=(jax.ShapeDtypeS...  76.3 us
    unnamed x2, local copies, waits for them, and re-layouts  3.19 us

profile of v2, /device:TPU:73, one launch (start us, length us, event | category | flops | bytes accessed | tf_op | source)
XLA Modules:
  0.0 80.8 jit_solution(6955269965296003702)
XLA Ops:
  1.3 76.3 %coupled_step.1 = (f32[8,32,512]{2,1,0:T(8,128)}, f32[8,1,512]{2,1,0:T(1,128)}) custom-call(s32[1,1,1]{2,1,0:T(1,128)S(6)} %copy.12.ncol_h, s32[1,1,1,7]{3,2,1,0:T(1,128)} %fcol_h.1, f32[8,32,512]{2,1,0:T(8,128)} %src_h.1, f32[8,16,32]{2,1,0:T(8,128)} %bitcast.7, s32[8,1,128]{2,1,0:T(1,128)} %ft_h.1, bf16[1024,1024]{1,0:T(8,128)(2,1)} %bitcast.4, ...), custom_call_target="tpu_custom_call" | custom-call | tf_op jit(solution)/shard_map/coupled_step/pallas_call | solution.py:786
  77.6 1.9 %copy.13 = f32[8,32,512]{2,1,0:T(8,128)} copy(f32[8,32,512]{2,1,0:T(8,128)} %get-tuple-element.4) | data formatting | bytes 1048576
  79.5 1.3 %copy.14 = f32[8,1,512]{2,1,0:T(1,128)} copy(f32[8,1,512]{2,1,0:T(1,128)} %get-tuple-element.5) | data formatting | bytes 32768

commit v3 on v2

--- a/solution.py
+++ b/solution.py
@@ -196,9 +196,10 @@
     lanes32 = lax.div(iota((DZ, L), 1), E)
 
     def pack(u, n):
-        if n == 1:
-            vxs[0] = u[1].astype(BF16)
-            vxs[1] = u[CX].astype(BF16)
+        if n > 0:
+            for side, x in enumerate((1, CX)):
+                edge = u[x] if n == 1 else u[x] - u1[x]
+                vxs[n - 1, side] = edge.astype(BF16)
 
         def step(k, c):
             low = jnp.zeros((DZ, L), F32)
@@ -378,8 +379,8 @@
 
             @pl.when(have)
             def _(side=side, dx=dx):
-                out = vxs.at[side] if n == 1 else u.at[1 + side * (CX - 1)]
-                there = vxr.at[1 - side] if n == 1 else u.at[(1 - side) * (CX + 1)]
+                out = vxs.at[n - 1, side] if n > 0 else u.at[1 + side * (CX - 1)]
+                there = vxr.at[n - 1, 1 - side] if n > 0 else u.at[(1 - side) * (CX + 1)]
                 act(
                     remote(
                         out, there,
@@ -408,10 +409,12 @@
 
             @pl.when(have)
             def _(side=side, dx=dx):
-                halo = vxr.at[side] if n == 1 else u.at[side * (CX + 1)]
+                halo = vxr.at[n - 1, side] if n > 0 else u.at[side * (CX + 1)]
                 remote(halo, halo, v_ss.at[n, side], v_rs.at[n, side], (gx + dx, gy, gz)).wait_recv()
-                if n == 1:
-                    u[side * (CX + 1)] = vxr[side].astype(F32)
+                if n > 0:
+                    edge = vxr[n - 1, side].astype(F32)
+                    x = side * (CX + 1)
+                    u[x] = edge if n == 1 else edge + u1[x]
 
         for side, have, dy in sides_y:
 
@@ -740,8 +743,8 @@
         pltpu.VMEM((2, 4, CX, L), F32),
         pltpu.VMEM((4, 1, L), F32),
         pltpu.VMEM((4, 1, L), F32),
-        pltpu.VMEM((2, DZ, W), BF16),
-        pltpu.VMEM((2, DZ, W), BF16),
+        pltpu.VMEM((2, 2, DZ, W), BF16),
+        pltpu.VMEM((2, 2, DZ, W), BF16),
         pltpu.VMEM((3, 2, CX // 4, DZ, L), F32),
         pltpu.VMEM((3, 2, CX // 4, DZ, L), F32),
         pltpu.VMEM((3, CX, 1, W), F32),

time: 81.1 us -> 74.9 us (0.924)
  the two profiles are of different devices: /device:TPU:73 before, /device:TPU:24 now
where the time goes in v3:
time: 74.9 us; the launch traced here: 73.9 us
  Pallas kernels  69.4 us (93%)
  local copies, waits for them, and re-layouts  3.19 us (4%)
  between operations  1.29 us (2%)
    pallas_call x1, Pallas kernels, body(): pl.pallas_call(functools.partial(kernel, cfg), out_shape=(jax.ShapeDtypeS...  69.4 us
    unnamed x2, local copies, waits for them, and re-layouts  3.19 us

profile of v3, /device:TPU:24, one launch (start us, length us, event | category | flops | bytes accessed | tf_op | source)
XLA Modules:
  0.0 73.9 jit_solution(3758252383579107335)
XLA Ops:
  1.3 69.4 %coupled_step.1 = (f32[8,32,512]{2,1,0:T(8,128)}, f32[8,1,512]{2,1,0:T(1,128)}) custom-call(s32[1,1,1]{2,1,0:T(1,128)S(6)} %copy.12.ncol_h, s32[1,1,1,7]{3,2,1,0:T(1,128)} %fcol_h.1, f32[8,32,512]{2,1,0:T(8,128)} %src_h.1, f32[8,16,32]{2,1,0:T(8,128)} %bitcast.7, s32[8,1,128]{2,1,0:T(1,128)} %ft_h.1, bf16[1024,1024]{1,0:T(8,128)(2,1)} %bitcast.4, ...), custom_call_target="tpu_custom_call" | custom-call | tf_op jit(solution)/shard_map/coupled_step/pallas_call | solution.py:789
  70.7 1.9 %copy.13 = f32[8,32,512]{2,1,0:T(8,128)} copy(f32[8,32,512]{2,1,0:T(8,128)} %get-tuple-element.4) | data formatting | bytes 1048576
  72.5 1.3 %copy.14 = f32[8,1,512]{2,1,0:T(1,128)} copy(f32[8,1,512]{2,1,0:T(1,128)} %get-tuple-element.5) | data formatting | bytes 32768

commit v4 on v2

--- a/solution.py
+++ b/solution.py
@@ -67,9 +67,9 @@
     ftr, cols_v, cols_s,
     pick, mask, faces, gath,
     near_v, near_p, onehot, u_v, u_p,
-    vparts, vblk, tsel, ns, nr, ws, wr, rs, rr,
-    load_sem, in_sem, x_ss, x_rs, c_ss, c_rs, v_ss, v_rs, ft_sem, col_ss, col_rs, smem_sem,
-    f_ss, f_rs, g_ss, g_rs, k_ss, k_rs, vp_ss, vp_rs, n_ss, n_rs, w_ss, w_rs, r_ss, r_rs,
+    vparts, vblk, tsel, ns, nr, ws, wr, rs, rr, rsb, rrb,
+    load_sem, in_sem, x_ss, x_rs, c_ss, c_rs, v_ss, v_rs, vx_ss, vx_rs, ft_sem, col_ss, col_rs, smem_sem,
+    f_ss, f_rs, g_ss, g_rs, k_ss, k_rs, vp_ss, vp_rs, n_ss, n_rs, w_ss, w_rs, r_ss, r_rs, b_ss, b_rs,
 ):
     n_gx, n_gy, far, rank, total_y = cfg
     tile = CX * total_y
@@ -195,11 +195,18 @@
 
     lanes32 = lax.div(iota((DZ, L), 1), E)
 
+    def pack_x(slot):
+        for side, x in enumerate((1, CX)):
+            if slot == 0:
+                coarse = u1[x].astype(BF16)
+                vxs[0, side] = coarse
+                vxs[1, side] = (u1[x] - coarse.astype(F32)).astype(BF16)
+            elif slot == 2:
+                vxs[2, side] = u2[x].astype(BF16)
+            else:
+                vxs[3, side] = (u3[x] - u1[x]).astype(BF16)
+
     def pack(u, n):
-        if n == 1:
-            vxs[0] = u[1].astype(BF16)
-            vxs[1] = u[CX].astype(BF16)
-
         def step(k, c):
             low = jnp.zeros((DZ, L), F32)
             high = jnp.zeros((DZ, L), F32)
@@ -221,6 +228,7 @@
 
         lax.fori_loop(0, CX, zstep, 0)
 
+    pack_x(0)
     pack(u1, 0)
 
     for side, have in ((0, low_x), (1, high_x)):
@@ -372,22 +380,42 @@
 
     fields = (u1, u2, u3)
 
-    def vol_send(n, act):
-        u = fields[n]
+    def vol_x(slot, act):
         for side, have, dx in sides:
 
             @pl.when(have)
             def _(side=side, dx=dx):
-                out = vxs.at[side] if n == 1 else u.at[1 + side * (CX - 1)]
-                there = vxr.at[1 - side] if n == 1 else u.at[(1 - side) * (CX + 1)]
                 act(
                     remote(
-                        out, there,
-                        v_ss.at[n, side], v_rs.at[n, 1 - side], (gx + dx, gy, gz),
+                        vxs.at[slot, side], vxr.at[slot, 1 - side],
+                        vx_ss.at[slot, side], vx_rs.at[slot, 1 - side], (gx + dx, gy, gz),
                     ),
                     0,
                 )
 
+    def vol_x_recv(slot):
+        for side, have, dx in sides:
+
+            @pl.when(have)
+            def _(side=side, dx=dx):
+                halo = vxr.at[slot, side]
+                remote(
+                    halo, halo, vx_ss.at[slot, side], vx_rs.at[slot, side], (gx + dx, gy, gz)
+                ).wait_recv()
+                value = vxr[slot, side].astype(F32)
+                rim = side * (CX + 1)
+                edge = side * (CX - 1)
+                if slot == 0:
+                    u1[rim] = value
+                elif slot == 1:
+                    u1[rim] = u1[rim] + value
+                    u2[edge + 1] = u2[edge + 1] + rinv[edge] * value
+                elif slot == 2:
+                    u2[rim] = value + rinv[edge] * vxs[1, side].astype(F32)
+                else:
+                    u3[rim] = u1[rim] + value
+
+    def vol_send(n, act):
         for side, have, dy in sides_y:
 
             @pl.when(have)
@@ -403,16 +431,6 @@
         act(remote(vzs.at[n], vzr.at[n], v_ss.at[n, 4], v_rs.at[n, 4], (gx, gy, other)), 0)
 
     def vol_recv(n):
-        u = fields[n]
-        for side, have, dx in sides:
-
-            @pl.when(have)
-            def _(side=side, dx=dx):
-                halo = vxr.at[side] if n == 1 else u.at[side * (CX + 1)]
-                remote(halo, halo, v_ss.at[n, side], v_rs.at[n, side], (gx + dx, gy, gz)).wait_recv()
-                if n == 1:
-                    u[side * (CX + 1)] = vxr[side].astype(F32)
-
         for side, have, dy in sides_y:
 
             @pl.when(have)
@@ -424,6 +442,7 @@
 
         remote(vzr.at[n], vzr.at[n], v_ss.at[n, 4], v_rs.at[n, 4], (gx, gy, other)).wait_recv()
 
+    vol_x(0, start)
     vol_send(0, start)
 
     def tables(table, slot):
@@ -502,6 +521,7 @@
 
     each(ring, lambda k: f_send(k).start())
 
+    vol_x(1, start)
     each(team, lambda d: vp_send(d).start())
 
     remote(ft, ftr, ft_sem.at[0], ft_sem.at[1], (anti, gy, gz)).wait_recv()
@@ -580,8 +600,13 @@
     each(nq, lambda d: g_send(d).start())
     k_send(0).start()
 
+    vol_x_recv(0)
     vol_recv(0)
     sweep(0, keep(u2))
+    pack_x(2)
+    vol_x(2, start)
+
+    vol_x_recv(1)
     pack(u2, 1)
     vol_send(1, start)
 
@@ -648,8 +673,11 @@
     each(team, weights_out)
     wr[seat] = partial_weights(seat)
 
+    vol_x_recv(2)
     vol_recv(1)
     sweep(1, keep(u3))
+    pack_x(3)
+    vol_x(3, start)
     pack(u3, 2)
     vol_send(2, start)
 
@@ -663,17 +691,38 @@
     acc = acc + dot_nn(weights.astype(BF16), u_p[...])
     for j in range(n_gy):
         rs[j] = acc[:, j * L : (j + 1) * L]
+        rsb[j] = acc[:, j * L : (j + 1) * L].astype(BF16)
 
     def r_send(d):
-        t = peer(d)
-        return remote(rs.at[t], rr.at[gy], r_ss.at[d], r_rs.at[d], (gx, t, gz))
+        t = mate(d)
+        return remote(rs.at[bench + t], rr.at[seat], r_ss.at[d], r_rs.at[d], (gx, bench + t, gz))
 
     def r_recv(d):
-        s = source_of(d)
-        return remote(rr.at[s], rr.at[s], r_ss.at[d], r_rs.at[d], (gx, s, gz))
-
-    each(n_gy, lambda d: r_send(d).start())
-    rr[gy] = rs[gy]
+        s = mate_from(d)
+        return remote(rr.at[s], rr.at[s], r_ss.at[d], r_rs.at[d], (gx, bench + s, gz))
+
+    def b_send(k):
+        step = team * (lax.div(k, team) + 1)
+        t = lax.rem(bench + step, n_gy) + lax.rem(k, team)
+        return remote(
+            rsb.at[t], rrb.at[step - team + seat], b_ss.at[k], b_rs.at[step - team + seat], (gx, t, gz)
+        )
+
+    def b_recv(k):
+        step = team * (lax.div(k, team) + 1)
+        s = lax.rem(bench + n_gy - step, n_gy) + lax.rem(k, team)
+        return remote(rrb.at[k], rrb.at[k], b_ss.at[k], b_rs.at[k], (gx, s, gz))
+
+    def across(f):
+        def step(k, c):
+            f(k)
+            return c
+
+        lax.fori_loop(0, n_gy - team, step, 0)
+
+    across(lambda k: b_send(k).start())
+    each(team, lambda d: r_send(d).start())
+    rr[seat] = rs[gy]
 
     def hold(x, total):
         sol[x] = total
@@ -692,12 +741,18 @@
     each(team, lambda d: w_send(d).wait_send())
     for n in range(3):
         vol_send(n, sent)
+    for n in range(4):
+        vol_x(n, sent)
+    vol_x_recv(3)
     vol_recv(2)
     sweep(2, hold)
-    each(n_gy, lambda d: r_recv(d).wait_recv())
+    each(team, lambda d: r_recv(d).wait_recv())
+    across(lambda k: b_recv(k).wait_recv())
     total = rr[0]
-    for j in range(1, n_gy):
+    for j in range(1, team):
         total = total + rr[j]
+    for j in range(n_gy - team):
+        total = total + rrb[j].astype(F32)
     widen = (iota((E, W), 0) == lax.rem(iota((E, W), 1), E)).astype(F32)
     wide = jnp.dot(total.T, widen, precision=HIGHEST, preferred_element_type=F32)
     keep_cell = lax.rem(iota((L, W), 0), YC) == lax.div(iota((L, W), 1), E)
@@ -708,7 +763,8 @@
         flux[x] = line
         sol[x] = (sol[x] + jnp.where(rows32 == face_z, line, 0.0)) * rinv[x]
 
-    each(n_gy, lambda d: r_send(d).wait_send())
+    each(team, lambda d: r_send(d).wait_send())
+    across(lambda k: b_send(k).wait_send())
 
 
 def body(source, coef, face_trace, near_col, far_col, near_tile, far_u, far_v):
@@ -740,8 +796,8 @@
         pltpu.VMEM((2, 4, CX, L), F32),
         pltpu.VMEM((4, 1, L), F32),
         pltpu.VMEM((4, 1, L), F32),
-        pltpu.VMEM((2, DZ, W), BF16),
-        pltpu.VMEM((2, DZ, W), BF16),
+        pltpu.VMEM((4, 2, DZ, W), BF16),
+        pltpu.VMEM((4, 2, DZ, W), BF16),
         pltpu.VMEM((3, 2, CX // 4, DZ, L), F32),
         pltpu.VMEM((3, 2, CX // 4, DZ, L), F32),
         pltpu.VMEM((3, CX, 1, W), F32),
@@ -766,18 +822,22 @@
         pltpu.VMEM((team, E, L), F32),
         pltpu.VMEM((team, E, L), F32),
         pltpu.VMEM((n_gy, E, L), F32),
-        pltpu.VMEM((n_gy, E, L), F32),
+        pltpu.VMEM((team, E, L), F32),
+        pltpu.VMEM((n_gy, E, L), BF16),
+        pltpu.VMEM((n_gy, E, L), BF16),
         dma((3,)),
         dma((5,)),
         dma((4,)), dma((4,)),
         dma((4,)), dma((4,)),
         dma((3, 5)), dma((3, 5)),
+        dma((4, 2)), dma((4, 2)),
         dma((2,)),
         dma((n_gy,)), dma((n_gy,)),
         dma,
         dma((ring,)), dma((ring,)),
         dma((nq,)), dma((nq,)),
         dma((nq,)), dma((nq,)),
+        dma((n_gy,)), dma((n_gy,)),
         dma((n_gy,)), dma((n_gy,)),
         dma((n_gy,)), dma((n_gy,)),
         dma((n_gy,)), dma((n_gy,)),

time: 81.1 us -> 73.6 us (0.908)
  the two profiles are of different devices: /device:TPU:73 before, /device:TPU:120 now
where the time goes in v4:
time: 73.6 us; the launch traced here: 73.3 us
  Pallas kernels  68.8 us (93%)
  local copies, waits for them, and re-layouts  3.19 us (4%)
  between operations  1.29 us (2%)
    pallas_call x1, Pallas kernels, body(): pl.pallas_call(functools.partial(kernel, cfg), out_shape=(jax.ShapeDtypeS...  68.8 us
    unnamed x2, local copies, waits for them, and re-layouts  3.19 us

profile of v4, /device:TPU:120, one launch (start us, length us, event | category | flops | bytes accessed | tf_op | source)
XLA Modules:
  0.0 73.3 jit_solution(17516330773800204751)
XLA Ops:
  1.3 68.8 %coupled_step.1 = (f32[8,32,512]{2,1,0:T(8,128)}, f32[8,1,512]{2,1,0:T(1,128)}) custom-call(s32[1,1,1]{2,1,0:T(1,128)S(6)} %copy.12.ncol_h, s32[1,1,1,7]{3,2,1,0:T(1,128)} %fcol_h.1, f32[8,32,512]{2,1,0:T(8,128)} %src_h.1, f32[8,16,32]{2,1,0:T(8,128)} %bitcast.7, s32[8,1,128]{2,1,0:T(1,128)} %ft_h.1, bf16[1024,1024]{1,0:T(8,128)(2,1)} %bitcast.4, ...), custom_call_target="tpu_custom_call" | custom-call | tf_op jit(solution)/shard_map/coupled_step/pallas_call | solution.py:846
  70.1 1.9 %copy.13 = f32[8,32,512]{2,1,0:T(8,128)} copy(f32[8,32,512]{2,1,0:T(8,128)} %get-tuple-element.4) | data formatting | bytes 1048576
  72.0 1.3 %copy.14 = f32[8,1,512]{2,1,0:T(1,128)} copy(f32[8,1,512]{2,1,0:T(1,128)} %get-tuple-element.5) | data formatting | bytes 32768
